TPU v7x, 32 devices: a whole 2x2x4 slice. The times are simulated.
32 devices in a mesh: gx: 16 (over z, y, core), gy: 2 (over x).
Axes of the slice: x: 2, y: 2, z: 4, core: 2. Of those that a mesh axis runs over, the one named last changes fastest.
Arguments:
- velocity: float32 [3, 256, 32, 128], P(None, 'gx', 'gy'), may hold values from -6 to 6
- pressure: float32 [256, 32, 128], P('gx', 'gy'), may hold values from -6 to 6
- land_type: int32 [256, 32], P('gx', 'gy'), may hold values from 0 to 15
- turbine_cells: int32 [256, 32, 128], P('gx', 'gy'), may hold values 0 or 1
- surface_drag: float32 [16], replicated, may hold values from 0.2 to 2
Outputs:
- velocity_new: float32 [3, 256, 32, 128], P(None, 'gx', 'gy')
- pressure_new: float32 [256, 32, 128], P('gx', 'gy')
All inputs are finite; a program needn't handle non-finite values. No bound on the sum of `turbine_cells` on one device may be relied on, other than what follows from the above.
Results may differ from a plain program's by a relative error of at most 0.00002.
Values sent between devices are 32-bit elements; how exact they have to be, the bound alone decides.
A program may use at most 64 MiB of HBM per device.

v0:
```python
import functools

import jax
import jax.numpy as jnp
from jax import lax
from jax.experimental import pallas as pl
from jax.experimental.pallas import tpu as pltpu
from jax.sharding import PartitionSpec as P

MESH = pl.DeviceIdType.MESH
F32 = jnp.float32
STEP = 0.1
WEIGHT = 0.8 / 12.0
KEEP = 0.2
OFF = 3
G_STRESS = 4
G_FINE = 8
VMEM_LIMIT = 24000 * 1024
REACH = 4


def loop(low, high, body, group):
    def run(indices):
        found = [store for index in indices for store in body(index)]
        for ref, at, value in found:
            ref[at] = value

    whole = (high - low) // group
    if whole == 1:
        run(range(low, low + group))
    elif whole > 1:

        def step(index, carry):
            run([low + index * group + k for k in range(group)])
            return carry

        lax.fori_loop(0, whole, step, 0)
    if low + whole * group < high:
        run(range(low + whole * group, high))


def kernel(
    nx, ny, vel_in, pre_in, turb_in, land_in, coeff_in, vel_out, pre_out,
    W, WLO, WHI, WSL, WSH, D, DLO, DHI, DSL, DSH, PA, PLO, PHI, PSL, PSH,
    PB, PC, CLO, CHI, CSL, CSH, F, FLO, FHI, FSL, FSH, T, S, tmp, tmp2, turb, land, coeff,
    G1, F1, P1A, P1B, G2, F2, P2A, P2B, F3, P3A, P3B, E1, E0,
    load_sem, send_sem, recv_sem,
):
    me_x, me_y = lax.axis_index("gx"), lax.axis_index("gy")
    own_x, own_y, nz = pre_out.shape
    side = (own_y // 8 + 1) * 8
    rows = own_x + 2 * OFF

    loads = [
        pltpu.make_async_copy(vel_in, W.at[:, OFF : OFF + own_x, 0:own_y], load_sem.at[0]),
        pltpu.make_async_copy(pre_in, PA.at[OFF : OFF + own_x, 0:own_y], load_sem.at[1]),
        pltpu.make_async_copy(turb_in, turb, load_sem.at[2]),
        pltpu.make_async_copy(land_in, land, load_sem.at[3]),
        pltpu.make_async_copy(coeff_in, coeff, load_sem.at[4]),
    ]
    for load in loads:
        load.start()

    def device(dx, dy):
        return (lax.rem(me_x + dx + nx, nx), lax.rem(me_y + dy + ny, ny))

    friends = [(dx, 0) for dx in range(-REACH, REACH + 1) if dx != 0]
    friends += [(dx, dy) for dx in (-1, 0, 1) for dy in range(1, ny)]
    close = [(dx, dy) for dx, dy in friends if abs(dx) < 2]
    barrier = pltpu.get_barrier_semaphore()
    for dx, dy in close:
        pl.semaphore_signal(barrier, inc=1, device_id=device(dx, dy), device_id_type=MESH)

    used = [0]

    def remote(src, dst, where):
        slot = used[0]
        used[0] += 1
        copy = pltpu.make_async_remote_copy(
            src_ref=src, dst_ref=dst, send_sem=send_sem.at[slot], recv_sem=recv_sem.at[slot],
            device_id=where, device_id_type=MESH,
        )
        copy.start()
        return copy

    def spans(dx, width, base):
        if dx == 0:
            return pl.ds(base, own_x), pl.ds(base, own_x)
        if dx == 1:
            return pl.ds(base + own_x - width, width), pl.ds(base - width, width)
        return pl.ds(base, width), pl.ds(base + own_x, width)

    def pick(ref, span, lead):
        return ref.at[:, span] if lead else ref.at[span]

    def send_x(M, width, lead=False):
        copies = []
        for dx in (1, -1):
            src, dst = spans(dx, width, OFF)
            a = M.at[:, src, 0:own_y] if lead else M.at[src, 0:own_y]
            b = M.at[:, dst, 0:own_y] if lead else M.at[dst, 0:own_y]
            copies.append(remote(a, b, device(dx, 0)))
        return copies

    def send_y(M, LO, HI, SL, SH, width, lead=False):
        if lead:
            SL[...] = M[:, OFF : OFF + own_x, own_y - width : own_y, :]
            SH[...] = M[:, OFF : OFF + own_x, 0:width, :]
        else:
            SL[...] = M[OFF : OFF + own_x, own_y - width : own_y, :]
            SH[...] = M[OFF : OFF + own_x, 0:width, :]
        copies = []
        for dx in (0, 1, -1):
            src, dst = spans(dx, width, width)
            if dx == 0:
                src = pl.ds(0, own_x)
            elif dx == 1:
                src = pl.ds(own_x - width, width)
            else:
                src = pl.ds(0, width)
            copies.append(remote(pick(SL, src, lead), pick(LO, dst, lead), device(dx, 1)))
            copies.append(remote(pick(SH, src, lead), pick(HI, dst, lead), device(dx, -1)))
        return copies

    def finish(copies):
        for copy in copies:
            copy.wait()

    def place(M, LO, HI, width, lead=False):
        lo, hi = OFF - width, OFF + own_x + width
        if lead:
            M[:, lo:hi, own_y : own_y + width, :] = HI[...]
            M[:, lo:hi, side - width : side, :] = LO[...]
        else:
            M[lo:hi, own_y : own_y + width, :] = HI[...]
            M[lo:hi, side - width : side, :] = LO[...]

    def lane_of(count):
        return lax.broadcasted_iota(jnp.int32, (count, nz), 1)

    def roll(v, shift, axis):
        return pltpu.roll(v, shift % v.shape[axis], axis)

    shape = (own_y, own_y)
    diagonal = lax.broadcasted_iota(jnp.int32, shape, 0) == lax.broadcasted_iota(jnp.int32, shape, 1)
    lane16 = lane_of(own_y)
    loads[3].wait()
    loads[4].wait()
    kinds = land[...]
    ground = jnp.zeros(kinds.shape, F32)
    for kind in range(coeff.shape[0]):
        ground = jnp.where(kinds == kind, coeff[kind], ground)
    loads[2].wait()
    for x in range(own_x):
        column = jnp.sum(jnp.where(diagonal, ground[x : x + 1, :], 0.0), axis=1, keepdims=True)
        low = jnp.where(lane16 == 0, column, 0.0)
        D[OFF + x, 0:own_y, :] = 2.0 * turb[x].astype(F32) + low
    loads[0].wait()
    loads[1].wait()
    pl.semaphore_wait(barrier, len(close))
    w_copies = send_y(W, WLO, WHI, WSL, WSH, 3, True) + send_x(W, 3, True)
    d_copies = send_y(D, DLO, DHI, DSL, DSH, 1) + send_x(D, 1)
    p_copies = send_y(PA, PLO, PHI, PSL, PSH, 3) + send_x(PA, 3)
    finish(w_copies)
    place(W, WLO, WHI, 3, True)
    finish(d_copies)
    place(D, DLO, DHI, 1)

    lane = lane_of(side)
    first, last = lane == 0, lane == nz - 1

    def up0(v):
        return jnp.where(last, 0.0, roll(v, -1, 1))

    def down0(v):
        return jnp.where(first, 0.0, roll(v, 1, 1))

    def stress_row(r):
        v = [W[a, r] for a in range(3)]
        gx = [0.5 * (W[a, r + 1] - W[a, r - 1]) for a in range(3)]
        gy = [0.5 * (roll(v[a], -1, 0) - roll(v[a], 1, 0)) for a in range(3)]
        gz = [up0(v[a]) - down0(v[a]) for a in range(3)]
        e01, e02, e12 = gx[1] + gy[0], gx[2] + gz[0], gy[2] + gz[1]
        q = 2.0 * (gx[0] * gx[0] + gy[1] * gy[1] + gz[2] * gz[2]) + e01 * e01 + e02 * e02 + e12 * e12
        visc = 0.03 * jnp.sqrt(q)
        twice = visc + visc
        t00, t11, t22 = twice * gx[0], twice * gy[1], twice * gz[2]
        t01, t02, t12 = visc * e01, visc * e02, visc * e12
        flat = v[0] * v[0] + v[1] * v[1]
        ghost = 0.03 * jnp.sqrt(2.0 * v[2] * v[2] + flat)
        ghosts = [ghost * v[0], ghost * v[1], (ghost + ghost) * v[2]]
        out = [(T, (0, r), t00), (T, (1, r), t01), (T, (2, r), t02)]
        drag = D[r] * jnp.sqrt(flat)
        for a, (ty, tz) in enumerate(((t01, t02), (t11, t12), (t12, t22))):
            change = 0.5 * (roll(ty, -1, 0) - roll(ty, 1, 0))
            change += jnp.where(last, -ghosts[a], roll(tz, -1, 1)) - jnp.where(first, ghosts[a], roll(tz, 1, 1))
            change -= v[0] * gx[a] + v[1] * gy[a] + v[2] * gz[a]
            if a < 2:
                change -= drag * v[a]
            if a == 0:
                change += 1.0
            out.append((S, (a, r), v[a] + STEP * change))
        return out

    loop(1, rows - 1, stress_row, G_STRESS)

    def star_row(r):
        return [
            (S, (a, r), S[a, r] + (0.5 * STEP) * (T[a, r + 1] - T[a, r - 1])) for a in range(3)
        ]

    loop(2, rows - 2, star_row, G_FINE)

    def source_row(r):
        s1, s2 = S[1, r], S[2, r]
        flat = 0.5 * (S[0, r + 1] - S[0, r - 1] + roll(s1, -1, 0) - roll(s1, 1, 0))
        return [(F, r, (flat + up0(s2) - down0(s2)) / STEP)]

    loop(OFF, OFF + own_x, source_row, G_FINE)
    f_copies = send_y(F, FLO, FHI, FSL, FSH, 2) + send_x(F, 2)
    finish(p_copies)
    place(PA, PLO, PHI, 3)
    finish(f_copies)
    place(F, FLO, FHI, 2)

    def stencil(src, r, sy, sz):
        p = src[r]
        lanes = lane_of(p.shape[0])
        z = jnp.where(lanes >= nz - sz, p, roll(p, -sz, 1)) + jnp.where(lanes < sz, p, roll(p, sz, 1))
        s = src[r + 1] + src[r - 1] + roll(p, -sy, 0) + roll(p, sy, 0)
        return p, s + 4.0 * z

    def sweep(src, dst, f, low, high, sy, sz, group=64):
        def body(r):
            p, around = stencil(src, r, sy, sz)
            return [(dst, r, KEEP * p + WEIGHT * (around - f[r]))]

        loop(low, high, body, min(group, high - low))

    def residual(src, f, r, sy, sz):
        p, around = stencil(src, r, sy, sz)
        return f[r] - (around - 12.0 * p)

    def pair(v, stride, axis):
        at = lax.broadcasted_iota(jnp.int32, v.shape, axis)
        even = (at // stride) % 2 == 0
        return v + jnp.where(even, roll(v, -stride, axis), roll(v, stride, axis))

    def spread(v, stride, bit):
        at = (lane_of(v.shape[0]) // stride) % 2
        return jnp.where(at == bit, v, roll(v, stride if bit == 0 else -stride, 1))

    sweep(PA, PB, F, 1, rows - 1, 1, 1, G_FINE)
    sweep(PB, PA, F, 2, rows - 2, 1, 1, G_FINE)
    PC[OFF : OFF + own_x, 0:own_y, :] = PA[OFF : OFF + own_x, 0:own_y, :]

    half = own_x // 2
    y1 = own_y // 2

    def fine_residual(i):
        r = OFF + 2 * i
        v = residual(PA, F, r, 1, 1) + residual(PA, F, r + 1, 1, 1)
        return [(tmp, i, pair(v[0:own_y], 1, 1))]

    loop(0, half, fine_residual, 2)
    packed = half // 2
    lane8 = lane_of(y1)
    for i in range(packed):
        parts = []
        for x in (2 * i, 2 * i + 1):
            parts.append(0.5 * (tmp[x, pl.ds(0, y1, 2), :] + tmp[x, pl.ds(1, y1, 2), :]))
        G1[0, 3 + i] = jnp.where(lane8 % 2 == 0, parts[0], parts[1])
    g_copies = []
    for dx in (1, -1, 0):
        for dy in range(ny):
            if dx == 0 and dy == 0:
                continue
            if dx == 0:
                src, dst = pl.ds(3, packed), pl.ds(3, packed)
            elif dx == 1:
                src, dst = pl.ds(packed, 3), pl.ds(0, 3)
            else:
                src, dst = pl.ds(3, 3), pl.ds(3 + packed, 3)
            g_copies.append(remote(G1.at[0, src], G1.at[(ny - dy) % ny, dst], device(dx, dy)))
    c_copies = send_y(PC, CLO, CHI, CSL, CSH, 3) + send_x(PC, 3)
    finish(g_copies)
    rows1 = 2 * (packed + 6)
    for k in range(ny):
        for j in range(packed + 6):
            v = G1[k, j]
            for bit in (0, 1):
                f = spread(v, 1, bit)
                F1[2 * j + bit, k * y1 : (k + 1) * y1, :] = f
                P1A[2 * j + bit, k * y1 : (k + 1) * y1, :] = -WEIGHT * f
    sweep(P1A, P1B, F1, 1, rows1 - 1, 1, 2)
    quarter = half // 2
    y2 = ny * y1 // 2
    lane2 = lane_of(y2)
    gathered = None
    for i in range(quarter):
        r = 6 + 2 * i
        tmp2[i] = pair(residual(P1B, F1, r, 1, 2) + residual(P1B, F1, r + 1, 1, 2), 2, 1)
        v = 0.5 * (tmp2[i, pl.ds(0, y2, 2), :] + tmp2[i, pl.ds(1, y2, 2), :])
        gathered = v if gathered is None else jnp.where(lane2 % 4 == i, v, gathered)
    G2[REACH] = gathered
    finish([remote(G2.at[REACH], G2.at[REACH - dx], device(dx, 0)) for dx, dy in friends if dy == 0])
    for s in range(2 * REACH + 1):
        v = G2[s]
        for b0 in (0, 1):
            u = spread(v, 1, b0)
            for b1 in (0, 1):
                f = spread(u, 2, b1)
                F2[4 * s + 2 * b1 + b0] = f
                P2A[4 * s + 2 * b1 + b0] = -WEIGHT * f
    rows2 = 4 * (2 * REACH + 1)
    sweep(P2A, P2B, F2, 1, rows2 - 1, 1, 4)

    def coarse_source(i):
        v = residual(P2B, F2, 2 * i, 1, 4) + residual(P2B, F2, 2 * i + 1, 1, 4)
        f = 0.5 * pair(pair(v, 4, 1), 1, 0)
        return [(F3, i, f), (P3A, i, -WEIGHT * f)]

    loop(1, rows2 // 2 - 1, coarse_source, rows2 // 2 - 2)
    sweep(P3A, P3B, F3, 2, 16, 2, 8)
    sweep(P3B, P3A, F3, 3, 15, 2, 8)
    sweep(P3A, P3B, F3, 4, 14, 2, 8)

    def line_row(r):
        mean = jnp.mean(residual(P3B, F3, r, 2, 8), axis=0, keepdims=True)
        v = P3B[r] - WEIGHT * mean
        return [(P2B, x, P2B[x] + v) for x in (2 * r, 2 * r + 1)]

    loop(6, 12, line_row, 6)
    sweep(P2B, P2A, F2, 13, 23, 1, 4)

    def second_row(m):
        p, around = stencil(P2A, m, 1, 4)
        v = KEEP * p + WEIGHT * (around - F2[m])
        E1[m - 14, pl.ds(0, y2, 2), :] = v
        E1[m - 14, pl.ds(1, y2, 2), :] = v
        e = E1[m - 14]
        r = 2 * (m - 13)
        P1B[r] = P1B[r] + e
        P1B[r + 1] = P1B[r + 1] + e

    for m in range(14, 22):
        second_row(m)
    sweep(P1B, P1A, F1, 3, 17, 1, 2)
    sweep(P1A, P1B, F1, 4, 16, 1, 2)
    finish(c_copies)
    place(PC, CLO, CHI, 3)
    full1 = ny * y1
    for m in range(4, 16):
        e = m - 4
        for shift in (0, 1):
            E0[e, pl.ds(shift, y1, 2), :] = P1B[m, 0:y1, :]
            E0[e, pl.ds(own_y + shift, 2, 2), :] = P1B[m, y1 : y1 + 2, :]
            E0[e, pl.ds(own_y + 4 + shift, 2, 2), :] = P1B[m, full1 - 2 : full1, :]
        for r in (2 * m - 9, 2 * m - 8):
            if 0 <= r < rows:
                PC[r] = PC[r] + E0[e]
    sweep(PC, PA, F, 1, rows - 1, 1, 1, G_FINE)
    sweep(PA, PB, F, 2, rows - 2, 1, 1, G_FINE)

    def out_row(x):
        r = OFF + x
        p = PB[r]
        out = [(pre_out, x, p[0:own_y])]
        gx = (0.5 * STEP) * (PB[r + 1] - PB[r - 1])
        gy = (0.5 * STEP) * (roll(p, -1, 0) - roll(p, 1, 0))
        gz = STEP * (jnp.where(last, p, roll(p, -1, 1)) - jnp.where(first, p, roll(p, 1, 1)))
        for a, g in enumerate((gx, gy, gz)):
            out.append((vel_out, (a, x), (S[a, r] - g)[0:own_y]))
        return out

    loop(0, own_x, out_row, 2)


def per_device(nx, ny, velocity, pressure, land_type, turbine_cells, surface_drag):
    _, own_x, own_y, nz = velocity.shape
    side = (own_y // 8 + 1) * 8
    rows = own_x + 2 * OFF
    window = pltpu.VMEM((rows, side, nz), F32)

    def rims(width, *lead):
        rim = pltpu.VMEM((*lead, own_x + 2 * width, width, nz), F32)
        stage = pltpu.VMEM((*lead, own_x, width, nz), F32)
        return [rim, rim, stage, stage]

    three = pltpu.VMEM((3, rows, side, nz), F32)
    half, quarter = own_x // 2, own_x // 4
    y1 = own_y // 2
    full1, full2 = ny * y1, ny * y1 // 2
    packed = half // 2
    level1 = pltpu.VMEM((2 * (packed + 6), full1, nz), F32)
    rows2 = quarter * (2 * REACH + 1)
    level2 = pltpu.VMEM((rows2, full2, nz), F32)
    level3 = pltpu.VMEM((rows2 // 2, full2, nz), F32)
    count = 5 * 8 + 3 * ny - 1 + 2 * REACH
    scratch = [three] + rims(3, 3) + [window] + rims(1) + [window] + rims(3)
    scratch += [window, window] + rims(3) + [window] + rims(2) + [three, three]
    scratch += [
        pltpu.VMEM((half, own_y, nz), F32),
        pltpu.VMEM((quarter, full1, nz), F32),
        pltpu.VMEM((own_x, own_y, nz), jnp.int32),
        pltpu.VMEM(land_type.shape, jnp.int32),
        pltpu.SMEM(surface_drag.shape, F32),
        pltpu.VMEM((ny, packed + 6, y1, nz), F32),
        level1, level1, level1,
        pltpu.VMEM((2 * REACH + 1, full2, nz), F32),
        level2, level2, level2, level3, level3, level3,
        pltpu.VMEM((8, full1, nz), F32),
        pltpu.VMEM((12, side, nz), F32),
        pltpu.SemaphoreType.DMA((5,)),
        pltpu.SemaphoreType.DMA((count,)),
        pltpu.SemaphoreType.DMA((count,)),
    ]
    inside = pl.BlockSpec(memory_space=pltpu.VMEM)
    velocity, pressure, land_type, turbine_cells, surface_drag = [pltpu.with_memory_space_constraint(a, pltpu.HBM) for a in (velocity, pressure, land_type, turbine_cells, surface_drag)]
    moved = tuple(
        pl.pallas_call(
            functools.partial(kernel, nx, ny),
            out_shape=(
                jax.ShapeDtypeStruct(velocity.shape, F32),
                jax.ShapeDtypeStruct(pressure.shape, F32),
            ),
            in_specs=[pl.BlockSpec(memory_space=pltpu.HBM)] * 5,
            out_specs=(inside, inside),
            scratch_shapes=scratch,
            compiler_params=pltpu.CompilerParams(
                collective_id=0, has_side_effects=True, vmem_limit_bytes=VMEM_LIMIT
            ),
        )(velocity, pressure, turbine_cells, land_type, surface_drag)
    )
    parts = 2
    vel_block = pl.BlockSpec((3, own_x // parts, own_y, nz), lambda i: (0, i, 0, 0))
    pre_block = pl.BlockSpec((own_x // parts, own_y, nz), lambda i: (i, 0, 0))
    return pl.pallas_call(
        hand_over,
        grid=(parts,),
        out_shape=(
            jax.ShapeDtypeStruct(velocity.shape, F32),
            jax.ShapeDtypeStruct(pressure.shape, F32),
        ),
        in_specs=[vel_block, pre_block],
        out_specs=(vel_block, pre_block), compiler_params=pltpu.CompilerParams(vmem_limit_bytes=VMEM_LIMIT),
    )(*moved)


def hand_over(vel_in, pre_in, vel_out, pre_out):
    vel_out[...] = vel_in[...]
    pre_out[...] = pre_in[...]


def solution(mesh):
    in_specs = (
        P(None, "gx", "gy", None),
        P("gx", "gy", None),
        P("gx", "gy"),
        P("gx", "gy", None),
        P(),
    )
    out_specs = (P(None, "gx", "gy", None), P("gx", "gy", None))
    body = functools.partial(per_device, mesh.shape["gx"], mesh.shape["gy"])
    return jax.shard_map(
        body, mesh=mesh, in_specs=in_specs, out_specs=out_specs, check_vma=False
    )
```

profile of v0, /device:TPU:0, one launch (start us, length us, event | category | flops | bytes accessed | tf_op | source)
XLA Modules:
  0.0 33.0 jit_solution(1422204058150399266)
XLA Ops:
  0.6 31.5 %shard_map.68 = (f32[3,16,16,128]{3,2,1,0:T(8,128)S(1)}, f32[16,16,128]{2,1,0:T(8,128)S(1)}) custom-call(f32[3,16,16,128]{3,2,1,0:T(8,128)} %vel_in.1, f32[16,16,128]{2,1,0:T(8,128)} %pre_in.1, s32[16,16,128]{2,1,0:T(8,128)} %turb_in.1, s32[16,16]{1,0:T(8,128)} %land_in.1, f32[16]{0:T(128)} %coeff_in.1), custom_call_target="tpu_custom_call" | custom-call | tf_op jit(solution)/shard_map/pallas_call | solution.py:421
  32.2 0.9 %shard_map.69 = (f32[3,16,16,128]{3,2,1,0:T(8,128)}, f32[16,16,128]{2,1,0:T(8,128)}) custom-call(f32[3,16,16,128]{3,2,1,0:T(8,128)S(1)} %get-tuple-element.4.vel_in, f32[16,16,128]{2,1,0:T(8,128)S(1)} %get-tuple-element.5.pre_in), custom_call_target="tpu_custom_call" | custom-call | tf_op jit(solution)/shard_map/pallas_call | solution.py:438
where the time goes:
time: 33.2 us; the launch traced here: 33 us
  Pallas kernels  32.4 us (98%)
  between operations  0.64 us (2%)
    pallas_call x1, Pallas kernels, per_device(): pl.pallas_call(functools.partial(kernel, nx, ny), out_shape=(jax.ShapeDty...  31.5 us
    pallas_call x1, Pallas kernels, per_device(): pl.pallas_call(hand_over, grid=(parts,), out_shape=(jax.ShapeDtypeStruct(...  0.86 us

commit v1 on v0

v1 whole, which is shorter than its diff:
```python
import functools

import jax
import jax.numpy as jnp
from jax import lax
from jax.experimental import pallas as pl
from jax.experimental.pallas import tpu as pltpu
from jax.sharding import PartitionSpec as P

MESH = pl.DeviceIdType.MESH
F32 = jnp.float32
STEP = 0.1
WEIGHT = 0.8 / 12.0
KEEP = 0.2
OFF = 3
RIM = 4
G_STRESS = 4
G_FINE = 8
VMEM_LIMIT = 24000 * 1024
REACH = 4


def loop(low, high, body, group):
    def run(indices):
        found = [store for index in indices for store in body(index)]
        for ref, at, value in found:
            ref[at] = value

    whole = (high - low) // group
    if whole == 1:
        run(range(low, low + group))
    elif whole > 1:

        def step(index, carry):
            run([low + index * group + k for k in range(group)])
            return carry

        lax.fori_loop(0, whole, step, 0)
    if low + whole * group < high:
        run(range(low + whole * group, high))


def lane_of(count, nz):
    return lax.broadcasted_iota(jnp.int32, (count, nz), 1)


def row_of(count, nz):
    return lax.broadcasted_iota(jnp.int32, (count, nz), 0)


def roll(v, shift, axis):
    return pltpu.roll(v, shift % v.shape[axis], axis)


def kernel(
    nx, ny, vel_in, pre_in, turb_in, land_in, coeff_in, S, PN,
    W, D, PA, F, T, R0, Z, ZA, ZB, X1, X2, A, Y1, tmp, tmp1, turb, land, coeff,
    H1, H1A, H1B, G1, F1, P1A, P1B, G2, F2, P2A, P2B, F3, P3A, P3B, E1, E0,
    load_sem, send_sem, recv_sem, token,
):
    me_x, me_y = lax.axis_index("gx"), lax.axis_index("gy")
    _, own_x, own_y, nz = vel_in.shape
    side = W.shape[2]
    rows = own_x + 2 * OFF
    half, quarter = own_x // 2, own_x // 4
    y1, y2 = own_y // 2, own_y // 4

    loads = [
        pltpu.make_async_copy(turb_in, turb, load_sem.at[0]),
        pltpu.make_async_copy(land_in, land, load_sem.at[1]),
        pltpu.make_async_copy(coeff_in, coeff, load_sem.at[2]),
        pltpu.make_async_copy(vel_in, W.at[:, OFF : OFF + own_x, 0:own_y], load_sem.at[3]),
        pltpu.make_async_copy(pre_in, PA.at[OFF : OFF + own_x, 0:own_y], load_sem.at[4]),
    ]

    def device(dx, dy):
        return (lax.rem(me_x + dx + nx, nx), lax.rem(me_y + dy + ny, ny))

    far = [(dx, dy) for dx in range(-REACH, REACH + 1) for dy in range(ny) if dx or dy]
    close = [(dx, dy) for dx, dy in far if abs(dx) < 2]
    barrier = pltpu.get_barrier_semaphore()
    for dx, dy in close:
        pl.semaphore_signal(barrier, inc=1, device_id=device(dx, dy), device_id_type=MESH)
    for load in loads:
        load.start()

    used = [0]

    def remote(src, dst, dx, dy):
        slot = used[0]
        used[0] += 1
        copy = pltpu.make_async_remote_copy(
            src_ref=src, dst_ref=dst, send_sem=send_sem.at[slot], recv_sem=recv_sem.at[slot],
            device_id=device(dx, dy), device_id_type=MESH,
        )
        copy.start()
        return copy

    def x_spans(dx, width, src_base, dst_base):
        if dx == 0:
            return slice(src_base, src_base + own_x), slice(dst_base, dst_base + own_x)
        if dx == 1:
            high = src_base + own_x
            return slice(high - width, high), slice(dst_base - width, dst_base)
        return slice(src_base, src_base + width), slice(dst_base + own_x, dst_base + own_x + width)

    def y_spans(dy, width):
        if dy == 0:
            return slice(0, own_y), slice(0, own_y)
        if dy == 1:
            return slice(own_y - width, own_y), slice(side - width, side)
        return slice(0, width), slice(own_y, own_y + width)

    def send(src, dst, src_base, dst_base, width, dx, dy, lead=False):
        sx, tx = x_spans(dx, width, src_base, dst_base)
        sy, ty = y_spans(dy, width)
        if lead:
            return remote(src.at[:, sx, sy], dst.at[:, tx, ty], dx, dy)
        return remote(src.at[sx, sy], dst.at[tx, ty], dx, dy)

    corners = [(dx, dy) for dx in (1, -1) for dy in (1, -1)]
    faces = [(0, 1), (0, -1), (1, 0), (-1, 0)]

    def finish(copies):
        for copy in copies:
            copy.wait()

    def tell(turn):
        for side_of, dx in enumerate((1, -1)):
            pl.semaphore_signal(
                token.at[turn, side_of], inc=1, device_id=device(dx, 0), device_id_type=MESH
            )

    def hear(turn):
        for side_of in range(2):
            pl.semaphore_wait(token.at[turn, side_of], 1)

    pl.semaphore_wait(barrier, len(close))
    w_copies = [send(vel_in, W, 0, OFF, 2, dx, dy, True) for dx, dy in corners]
    w_copies += [send(vel_in, W, 0, OFF, 3, dx, dy, True) for dx, dy in faces]
    p_copies = [send(pre_in, PA, 0, OFF, 1, dx, dy) for dx, dy in faces]
    shape = (own_y, own_y)
    diagonal = lax.broadcasted_iota(jnp.int32, shape, 0) == lax.broadcasted_iota(jnp.int32, shape, 1)
    lane16 = lane_of(own_y, nz)
    loads[1].wait()
    loads[2].wait()
    kinds = land[...]
    ground = jnp.zeros(kinds.shape, F32)
    for kind in range(coeff.shape[0]):
        ground = jnp.where(kinds == kind, coeff[kind], ground)
    loads[0].wait()
    for x in range(own_x):
        column = jnp.sum(jnp.where(diagonal, ground[x : x + 1, :], 0.0), axis=1, keepdims=True)
        low = jnp.where(lane16 == 0, column, 0.0)
        D[OFF + x, 0:own_y, :] = 2.0 * turb[x].astype(F32) + low
    d_copies = [send(D, D, OFF, OFF, 1, dx, dy) for dx, dy in faces]
    blank = jnp.zeros((side, nz), F32)
    for r in (1, 2, rows - 3, rows - 2):
        Z[r] = blank
    for r in (0, 1, rows - 2, rows - 1):
        ZA[r] = blank
    blank1 = jnp.zeros((2 * y1, nz), F32)
    for r in (1, 2, half + 5, half + 6):
        H1[r] = blank1
    for r in (0, 1, half + 6, half + 7):
        H1A[r] = blank1
    for r in (0, half + 7):
        H1B[r] = blank1
    loads[3].wait()
    loads[4].wait()
    finish(w_copies)
    tell(0)
    lane = lane_of(side, nz)
    first, last = lane == 0, lane == nz - 1

    def up0(v):
        return jnp.where(last, 0.0, roll(v, -1, 1))

    def down0(v):
        return jnp.where(first, 0.0, roll(v, 1, 1))

    def stress_row(r):
        v = [W[a, r] for a in range(3)]
        gx = [0.5 * (W[a, r + 1] - W[a, r - 1]) for a in range(3)]
        gy = [0.5 * (roll(v[a], -1, 0) - roll(v[a], 1, 0)) for a in range(3)]
        gz = [up0(v[a]) - down0(v[a]) for a in range(3)]
        e01, e02, e12 = gx[1] + gy[0], gx[2] + gz[0], gy[2] + gz[1]
        q = 2.0 * (gx[0] * gx[0] + gy[1] * gy[1] + gz[2] * gz[2]) + e01 * e01 + e02 * e02 + e12 * e12
        visc = 0.03 * jnp.sqrt(q)
        twice = visc + visc
        t00, t11, t22 = twice * gx[0], twice * gy[1], twice * gz[2]
        t01, t02, t12 = visc * e01, visc * e02, visc * e12
        flat = v[0] * v[0] + v[1] * v[1]
        ghost = 0.03 * jnp.sqrt(2.0 * v[2] * v[2] + flat)
        ghosts = [ghost * v[0], ghost * v[1], (ghost + ghost) * v[2]]
        out = [(T, (0, r), t00), (T, (1, r), t01), (T, (2, r), t02)]
        drag = D[r] * jnp.sqrt(flat)
        for a, (ty, tz) in enumerate(((t01, t02), (t11, t12), (t12, t22))):
            change = 0.5 * (roll(ty, -1, 0) - roll(ty, 1, 0))
            change += jnp.where(last, -ghosts[a], roll(tz, -1, 1)) - jnp.where(first, ghosts[a], roll(tz, 1, 1))
            change -= v[0] * gx[a] + v[1] * gy[a] + v[2] * gz[a]
            if a < 2:
                change -= drag * v[a]
            if a == 0:
                change += 1.0
            out.append((S, (a, r), v[a] + STEP * change))
        return out

    finish(d_copies)
    loop(1, rows - 1, stress_row, G_STRESS)
    hear(0)
    tell(1)

    def star_row(r):
        return [
            (S, (a, r), S[a, r] + (0.5 * STEP) * (T[a, r + 1] - T[a, r - 1])) for a in range(3)
        ]

    loop(2, rows - 2, star_row, G_FINE)
    finish(p_copies)

    def stencil(src, r, sy, sz):
        p = src[r]
        lanes = lane_of(p.shape[0], nz)
        z = jnp.where(lanes >= nz - sz, p, roll(p, -sz, 1)) + jnp.where(lanes < sz, p, roll(p, sz, 1))
        s = src[r + 1] + src[r - 1] + roll(p, -sy, 0) + roll(p, sy, 0)
        return p, s + 4.0 * z

    def smooth(src, r, sy, sz):
        p, around = stencil(src, r, sy, sz)
        return KEEP * p + WEIGHT * around

    def smooth_all(src, dst, low, high, sy, sz, group=64):
        loop(low, high, lambda r: [(dst, r, smooth(src, r, sy, sz))], min(group, high - low))

    def sweep(src, dst, f, low, high, sy, sz, group=64):
        def body(r):
            p, around = stencil(src, r, sy, sz)
            return [(dst, r, KEEP * p + WEIGHT * (around - f[r]))]

        loop(low, high, body, min(group, high - low))

    def residual(src, f, r, sy, sz):
        p, around = stencil(src, r, sy, sz)
        return f[r] - (around - 12.0 * p)

    own = row_of(side, nz) < own_y

    def source_row(r):
        s1, s2 = S[1, r], S[2, r]
        flat = 0.5 * (S[0, r + 1] - S[0, r - 1] + roll(s1, -1, 0) - roll(s1, 1, 0))
        f = (flat + up0(s2) - down0(s2)) / STEP
        p, around = stencil(PA, r, 1, 1)
        left = jnp.where(own, f - (around - 12.0 * p), 0.0)
        return [(Z, r, left), (R0, (r + RIM - OFF, slice(0, own_y)), left[0:own_y])]

    loop(OFF, OFF + own_x, source_row, G_FINE)
    r_copies = [send(R0, R0, RIM, RIM, 3, dx, dy) for dx, dy in corners]
    r_copies += [send(R0, R0, RIM, RIM, RIM, dx, dy) for dx, dy in faces]

    smooth_all(Z, ZA, 2, rows - 2, 1, 1, G_FINE)
    smooth_all(ZA, ZB, 1, rows - 1, 1, 1, G_FINE)

    def pair(v, stride, axis):
        at = lax.broadcasted_iota(jnp.int32, v.shape, axis)
        even = (at // stride) % 2 == 0
        return v + jnp.where(even, roll(v, -stride, axis), roll(v, stride, axis))

    def spread(v, stride, bit):
        at = (lane_of(v.shape[0], nz) // stride) % 2
        return jnp.where(at == bit, v, roll(v, stride if bit == 0 else -stride, 1))

    sub8 = row_of(y1, nz)

    def fine_residual(i):
        v = pair(ZB[2 * i + 1] + ZB[2 * i + 2], 1, 1)
        rim = 0.5 * v[own_y : own_y + 8]
        rim = jnp.where(sub8 == 0, rim + roll(rim, -1, 0), jnp.where(sub8 == 7, rim + roll(rim, 1, 0), 0.0))
        return [(tmp, i, v[0:own_y]), (H1, (i + 3, slice(y1, 2 * y1)), rim)]

    loop(0, half + 2, fine_residual, half + 2)
    for i in range(half + 2):
        H1[i + 3, 0:y1] = 0.5 * (tmp[i, pl.ds(0, y1, 2), :] + tmp[i, pl.ds(1, y1, 2), :])
    packs = half // 2
    lane1 = lane_of(2 * y1, nz)
    even1 = lane1 % 2 == 0
    for i in range(packs):
        G1[0, 1 + i] = jnp.where(even1, H1[4 + 2 * i], H1[5 + 2 * i])
    rim = jnp.where(even1, H1[half + 4], H1[3])
    G1[0, 0] = rim
    G1[0, packs + 1] = rim
    g_copies = []
    kept = 3
    for dx in (1, -1, 0):
        for dy in range(ny):
            if dx == 0 and dy == 0:
                continue
            k = (ny - dy) % ny
            if dx == 0:
                src, dst = pl.ds(0, packs + 1), pl.ds(0, packs + 1)
            elif dx == 1:
                src, dst = pl.ds(packs + 1 - kept, kept + 1), pl.ds(packs + 2, kept + 1)
            else:
                src, dst = pl.ds(0, kept + 1), pl.ds(packs + 3 + kept, kept + 1)
            g_copies.append(remote(G1.at[0, src], G1.at[k, dst], dx, dy))
    hear(1)
    smooth_all(H1, H1A, 2, half + 6, 1, 2)
    smooth_all(H1A, H1B, 1, half + 7, 1, 2)
    lane8 = lane_of(y1, nz)
    for j in range(quarter + 4):
        tmp1[j] = pair(H1B[2 * j] + H1B[2 * j + 1], 2, 1)
    for which, order in enumerate(((2, 3, 4, 5), (6, 7, 0, 1))):
        gathered = None
        for at, j in enumerate(order):
            v = 0.5 * (tmp1[j, pl.ds(0, y1, 2), :] + tmp1[j, pl.ds(1, y1, 2), :])
            gathered = v if gathered is None else jnp.where(lane8 % 4 == at, v, gathered)
        G2[0, REACH, which] = gathered
    h_copies = [
        remote(G2.at[0, REACH], G2.at[(ny - dy) % ny, REACH - dx], dx, dy) for dx, dy in far
    ]
    finish(r_copies)
    wide = own_x + 2 * RIM
    smooth_all(R0, X1, 1, wide - 1, 1, 1, G_FINE)
    smooth_all(X1, X2, 2, wide - 2, 1, 1, G_FINE)

    def base_row(r):
        total = R0[r] + X1[r] + X2[r] + smooth(X2, r, 1, 1)
        return [(A, r - 3, PA[r - RIM + OFF] - WEIGHT * total)]

    loop(3, wide - 3, base_row, G_FINE)
    finish(g_copies)
    full1 = ny * y1
    count1 = packs + 2 * kept

    def joined(k, q):
        if q < 0:
            v = G1[k, packs + 2 + q + kept]
            return v + jnp.where(even1, 0.0, G1[k, 0]) if q == -1 else v
        if q >= packs:
            v = G1[k, packs + 4 + kept + q - packs]
            return v + jnp.where(even1, G1[k, 0], 0.0) if q == packs else v
        v = G1[k, 1 + q]
        if q == 0:
            v = v + jnp.where(even1, G1[k, packs + 2 + kept], 0.0)
        if q == packs - 1:
            v = v + jnp.where(even1, 0.0, G1[k, packs + 3 + kept])
        return v

    for q in range(-kept, packs + kept):
        frames = [joined(k, q) for k in range(ny)]
        for k in range(ny):
            before, after = frames[(k - 1) % ny][y1:], frames[(k + 1) % ny][y1:]
            edge = before if ny == 2 else jnp.where(sub8 < y1 // 2, before, after)
            v = frames[k][0:y1] + edge
            for bit in (0, 1):
                f = spread(v, 1, bit)
                r = 2 * (q + kept) + bit
                F1[r, k * y1 : (k + 1) * y1, :] = f
                P1A[r, k * y1 : (k + 1) * y1, :] = -WEIGHT * f
    sweep(P1A, P1B, F1, 1, 2 * count1 - 1, 1, 2)
    finish(h_copies)
    full2 = ny * y2
    low2 = lane8 % 4 < 2
    blank8 = jnp.zeros((y1, nz), F32)

    def joined2(k, s):
        before = G2[k, s - 1, 1] if s > 0 else blank8
        after = G2[k, s + 1, 1] if s < 2 * REACH else blank8
        return G2[k, s, 0] + jnp.where(low2, before, after)

    for s in range(2 * REACH + 1):
        frames = [joined2(k, s) for k in range(ny)]
        turned = [roll(v, y2, 0) for v in frames]
        for m in range(ny // 2):
            k = 2 * m
            if ny == 2:
                v = frames[0] + turned[1]
            else:
                lower = frames[k] + jnp.where(sub8 < 2, turned[(k - 1) % ny], turned[(k + 1) % ny])
                upper = turned[k + 1] + jnp.where(sub8 < 6, frames[k], frames[(k + 2) % ny])
                v = jnp.where(sub8 < y2, lower, upper)
            for b0 in (0, 1):
                u = spread(v, 1, b0)
                for b1 in (0, 1):
                    f = spread(u, 2, b1)
                    F2[4 * s + 2 * b1 + b0, 8 * m : 8 * m + 8, :] = f
                    P2A[4 * s + 2 * b1 + b0, 8 * m : 8 * m + 8, :] = -WEIGHT * f
    rows2 = 4 * (2 * REACH + 1)
    sweep(P2A, P2B, F2, 1, rows2 - 1, 1, 4)

    def coarse_source(i):
        v = residual(P2B, F2, 2 * i, 1, 4) + residual(P2B, F2, 2 * i + 1, 1, 4)
        f = 0.5 * pair(pair(v, 4, 1), 1, 0)
        return [(F3, i, f), (P3A, i, -WEIGHT * f)]

    loop(1, rows2 // 2 - 1, coarse_source, rows2 // 2 - 2)
    sweep(P3A, P3B, F3, 2, 16, 2, 8)
    sweep(P3B, P3A, F3, 3, 15, 2, 8)
    sweep(P3A, P3B, F3, 4, 14, 2, 8)

    def line_row(r):
        mean = jnp.mean(residual(P3B, F3, r, 2, 8), axis=0, keepdims=True)
        v = P3B[r] - WEIGHT * mean
        return [(P2B, x, P2B[x] + v) for x in (2 * r, 2 * r + 1)]

    loop(6, 12, line_row, 6)
    sweep(P2B, P2A, F2, 13, 23, 1, 4)

    def second_row(m):
        p, around = stencil(P2A, m, 1, 4)
        v = KEEP * p + WEIGHT * (around - F2[m])
        E1[m - 14, pl.ds(0, full2, 2), :] = v
        E1[m - 14, pl.ds(1, full2, 2), :] = v
        e = E1[m - 14]
        r = 2 * (m - 13)
        P1B[r] = P1B[r] + e
        P1B[r + 1] = P1B[r + 1] + e

    for m in range(14, 22):
        second_row(m)
    sweep(P1B, P1A, F1, 3, 17, 1, 2)
    sweep(P1A, P1B, F1, 4, 16, 1, 2)
    for m in range(4, 16):
        e = m - 4
        for shift in (0, 1):
            E0[e, pl.ds(shift, y1, 2), :] = P1B[m, 0:y1, :]
            E0[e, pl.ds(own_y + shift, 2, 2), :] = P1B[m, y1 : y1 + 2, :]
            E0[e, pl.ds(own_y + 4 + shift, 2, 2), :] = P1B[m, full1 - 2 : full1, :]

    def first_pair(e):
        p = E0[e]
        z = jnp.where(last, p, roll(p, -1, 1)) + jnp.where(first, p, roll(p, 1, 1))
        base = (KEEP + WEIGHT) * p + WEIGHT * (roll(p, -1, 0) + roll(p, 1, 0) + 4.0 * z)
        return [
            (Y1, 2 * e - 2, base + WEIGHT * E0[e - 1]),
            (Y1, 2 * e - 1, base + WEIGHT * E0[e + 1]),
        ]

    loop(1, 11, first_pair, 5)
    loop(1, own_x + 3, lambda r: [(PN, r - 1, A[r - 1] + smooth(Y1, r, 1, 1))], 6)


def closing(S, PN, vel_out, pre_out, vel, pre, sem):
    _, own_x, own_y, nz = vel.shape
    lane = lane_of(PN.shape[1], nz)
    first, last = lane == 0, lane == nz - 1
    copies = []
    part = 4
    for low in range(0, own_x, part):
        for x in range(low, low + part):
            p = PN[x + 1]
            pre[x] = p[0:own_y]
            gx = (0.5 * STEP) * (PN[x + 2] - PN[x])
            gy = (0.5 * STEP) * (roll(p, -1, 0) - roll(p, 1, 0))
            gz = STEP * (jnp.where(last, p, roll(p, -1, 1)) - jnp.where(first, p, roll(p, 1, 1)))
            for a, g in enumerate((gx, gy, gz)):
                vel[a, x] = S[a, OFF + x, 0:own_y] - g[0:own_y]
        span = pl.ds(low, part)
        at = len(copies)
        copies.append(pltpu.make_async_copy(vel.at[:, span], vel_out.at[:, span], sem.at[at]))
        copies.append(pltpu.make_async_copy(pre.at[span], pre_out.at[span], sem.at[at + 1]))
        copies[-2].start()
        copies[-1].start()
    for copy in copies:
        copy.wait()


def per_device(nx, ny, velocity, pressure, land_type, turbine_cells, surface_drag):
    _, own_x, own_y, nz = velocity.shape
    side = (own_y // 8 + 1) * 8
    rows = own_x + 2 * OFF
    wide = own_x + 2 * RIM
    half, quarter = own_x // 2, own_x // 4
    y1 = own_y // 2
    full1, full2 = ny * y1, ny * y1 // 2
    packs = half // 2
    rows2 = quarter * (2 * REACH + 1)

    def window(*shape):
        return pltpu.VMEM((*shape, nz), F32)

    level1 = window(2 * (packs + 6), full1)
    level2 = window(rows2, full2)
    level3 = window(rows2 // 2, full2)
    frame1 = window(half + 8, 2 * y1)
    count = 8 + 4 + 4 + 8 + 3 * ny - 1 + (2 * REACH + 1) * ny - 1
    scratch = [
        window(3, rows, side), window(rows, side), window(rows, side), window(rows, side),
        window(3, rows, side), window(wide, side),
        window(rows, side), window(rows, side), window(rows, side),
        window(wide, side), window(wide, side), window(own_x + 2, side), window(own_x + 4, side),
        window(half + 2, own_y), window(quarter + 4, 2 * y1),
        pltpu.VMEM((own_x, own_y, nz), jnp.int32),
        pltpu.VMEM(land_type.shape, jnp.int32),
        pltpu.SMEM(surface_drag.shape, F32),
        frame1, frame1, frame1, window(ny, packs + 10, 2 * y1),
        level1, level1, level1,
        window(ny, 2 * REACH + 1, 2, y1),
        level2, level2, level2, level3, level3, level3,
        window(8, full1), window(12, side),
        pltpu.SemaphoreType.DMA((5,)),
        pltpu.SemaphoreType.DMA((count,)),
        pltpu.SemaphoreType.DMA((count,)),
        pltpu.SemaphoreType.REGULAR((2, 2)),
    ]
    inside = pl.BlockSpec(memory_space=pltpu.VMEM)
    outside = pl.BlockSpec(memory_space=pltpu.HBM)
    arguments = [
        pltpu.with_memory_space_constraint(a, pltpu.HBM)
        for a in (velocity, pressure, turbine_cells, land_type, surface_drag)
    ]
    star, middle = pl.pallas_call(
        functools.partial(kernel, nx, ny),
        out_shape=(
            jax.ShapeDtypeStruct((3, rows, side, nz), F32),
            jax.ShapeDtypeStruct((own_x + 2, side, nz), F32),
        ),
        in_specs=[outside] * 5,
        out_specs=(inside, inside),
        scratch_shapes=scratch,
        compiler_params=pltpu.CompilerParams(
            collective_id=0, has_side_effects=True, vmem_limit_bytes=VMEM_LIMIT
        ),
    )(*arguments)
    return pl.pallas_call(
        closing,
        out_shape=(
            jax.ShapeDtypeStruct(velocity.shape, F32),
            jax.ShapeDtypeStruct(pressure.shape, F32),
        ),
        in_specs=[inside, inside],
        out_specs=(outside, outside),
        scratch_shapes=[
            pltpu.VMEM(velocity.shape, F32),
            pltpu.VMEM(pressure.shape, F32),
            pltpu.SemaphoreType.DMA((2 * own_x // 4,)),
        ],
        compiler_params=pltpu.CompilerParams(vmem_limit_bytes=VMEM_LIMIT),
    )(star, middle)


def solution(mesh):
    in_specs = (
        P(None, "gx", "gy", None),
        P("gx", "gy", None),
        P("gx", "gy"),
        P("gx", "gy", None),
        P(),
    )
    out_specs = (P(None, "gx", "gy", None), P("gx", "gy", None))
    body = functools.partial(per_device, mesh.shape["gx"], mesh.shape["gy"])
    return jax.shard_map(
        body, mesh=mesh, in_specs=in_specs, out_specs=out_specs, check_vma=False
    )
```

time: 33.2 us -> 25.2 us (0.76)
  Pallas kernels: 32.4 us -> 24.4 us
    pallas_call x1, Pallas kernels: 31.5 us -> 23.5 us  [per_device(): pl.pallas_call(functools.partial(kernel, nx, ny), out_shape=(jax.ShapeDty...]
where the time goes in v1:
time: 25.2 us; the launch traced here: 25.1 us
  Pallas kernels  24.4 us (97%)
  between operations  0.64 us (3%)
    pallas_call x1, Pallas kernels, per_device(): pl.pallas_call(functools.partial(kernel, nx, ny), out_shape=(jax.ShapeDty...  23.5 us
    pallas_call x1, Pallas kernels, per_device(): pl.pallas_call(closing, out_shape=(jax.ShapeDtypeStruct(velocity.shape, F...  0.94 us

profile of v1, /device:TPU:0, one launch (start us, length us, event | category | flops | bytes accessed | tf_op | source)
XLA Modules:
  0.0 25.1 jit_solution(4415094698942918686)
XLA Ops:
  0.6 23.5 %shard_map.68 = (f32[3,22,24,128]{3,2,1,0:T(8,128)S(1)}, f32[18,24,128]{2,1,0:T(8,128)S(1)}) custom-call(f32[3,16,16,128]{3,2,1,0:T(8,128)} %vel_in.1, f32[16,16,128]{2,1,0:T(8,128)} %pre_in.1, s32[16,16,128]{2,1,0:T(8,128)} %turb_in.1, s32[16,16]{1,0:T(8,128)} %land_in.1, f32[16]{0:T(128)} %coeff_in.1), custom_call_target="tpu_custom_call" | custom-call | tf_op jit(solution)/shard_map/pallas_call | solution.py:512
  24.1 0.9 %shard_map.69 = (f32[3,16,16,128]{3,2,1,0:T(8,128)}, f32[16,16,128]{2,1,0:T(8,128)}) custom-call(f32[3,22,24,128]{3,2,1,0:T(8,128)S(1)} %get-tuple-element.4.S, f32[18,24,128]{2,1,0:T(8,128)S(1)} %get-tuple-element.5.PN), custom_call_target="tpu_custom_call" | custom-call | tf_op jit(solution)/shard_map/pallas_call | solution.py:525

commit v2 on v1

--- a/solution.py
+++ b/solution.py
@@ -1,4 +1,5 @@
 import functools
+import math
 
 import jax
 import jax.numpy as jnp
@@ -54,9 +55,9 @@
 
 def kernel(
     nx, ny, vel_in, pre_in, turb_in, land_in, coeff_in, S, PN,
-    W, D, PA, F, T, R0, Z, ZA, ZB, X1, X2, A, Y1, tmp, tmp1, turb, land, coeff,
-    H1, H1A, H1B, G1, F1, P1A, P1B, G2, F2, P2A, P2B, F3, P3A, P3B, E1, E0,
-    load_sem, send_sem, recv_sem, token,
+    W, D, PA, F, T, R0, Z, ZA, X1, X2, A, Y1, tmp, tmp1, turb, land, coeff,
+    H1, H1A, G1, F1, P1A, P1B, G2, F2, P2A, P2B, F3, P3A, P3B, E1, E0,
+    spare, load_sem, send_sem, recv_sem, token,
 ):
     me_x, me_y = lax.axis_index("gx"), lax.axis_index("gy")
     _, own_x, own_y, nz = vel_in.shape
@@ -84,17 +85,29 @@
     for load in loads:
         load.start()
 
-    used = [0]
-
-    def remote(src, dst, dx, dy):
-        slot = used[0]
-        used[0] += 1
-        copy = pltpu.make_async_remote_copy(
-            src_ref=src, dst_ref=dst, send_sem=send_sem.at[slot], recv_sem=recv_sem.at[slot],
+    groups, sent = [], []
+
+    def group():
+        groups.append(0)
+        return len(groups) - 1
+
+    def lines_of(ref):
+        return math.prod(ref.shape) // nz
+
+    def remote(src, dst, dx, dy, at):
+        groups[at] += lines_of(dst)
+        sent.append(lines_of(src))
+        pltpu.make_async_remote_copy(
+            src_ref=src, dst_ref=dst, send_sem=send_sem.at[0], recv_sem=recv_sem.at[at],
             device_id=device(dx, dy), device_id_type=MESH,
-        )
-        copy.start()
-        return copy
+        ).start()
+
+    def await_lines(sem, count):
+        part = spare.at[pl.ds(0, count)]
+        pltpu.make_async_copy(part, part, sem).wait()
+
+    def finish(at):
+        await_lines(recv_sem.at[at], groups[at])
 
     def x_spans(dx, width, src_base, dst_base):
         if dx == 0:
@@ -111,34 +124,45 @@
             return slice(own_y - width, own_y), slice(side - width, side)
         return slice(0, width), slice(own_y, own_y + width)
 
-    def send(src, dst, src_base, dst_base, width, dx, dy, lead=False):
+    def send(at, src, dst, src_base, dst_base, width, dx, dy, lead=False):
         sx, tx = x_spans(dx, width, src_base, dst_base)
         sy, ty = y_spans(dy, width)
         if lead:
-            return remote(src.at[:, sx, sy], dst.at[:, tx, ty], dx, dy)
-        return remote(src.at[sx, sy], dst.at[tx, ty], dx, dy)
+            remote(src.at[:, sx, sy], dst.at[:, tx, ty], dx, dy, at)
+        else:
+            remote(src.at[sx, sy], dst.at[tx, ty], dx, dy, at)
 
     corners = [(dx, dy) for dx in (1, -1) for dy in (1, -1)]
     faces = [(0, 1), (0, -1), (1, 0), (-1, 0)]
 
-    def finish(copies):
-        for copy in copies:
-            copy.wait()
-
     def tell(turn):
-        for side_of, dx in enumerate((1, -1)):
-            pl.semaphore_signal(
-                token.at[turn, side_of], inc=1, device_id=device(dx, 0), device_id_type=MESH
-            )
+        for dx in (1, -1):
+            pl.semaphore_signal(token.at[turn], inc=1, device_id=device(dx, 0), device_id_type=MESH)
 
     def hear(turn):
-        for side_of in range(2):
-            pl.semaphore_wait(token.at[turn, side_of], 1)
+        pl.semaphore_wait(token.at[turn], 2)
 
     pl.semaphore_wait(barrier, len(close))
-    w_copies = [send(vel_in, W, 0, OFF, 2, dx, dy, True) for dx, dy in corners]
-    w_copies += [send(vel_in, W, 0, OFF, 3, dx, dy, True) for dx, dy in faces]
-    p_copies = [send(pre_in, PA, 0, OFF, 1, dx, dy) for dx, dy in faces]
+    tell(0)
+    quart = own_x // 4
+    inner = (own_x - 2 * quart + 2) // 3
+    cuts = [(0, quart), (own_x - quart, own_x)]
+    cuts += [(low, min(low + inner, own_x - quart)) for low in range(quart, own_x - quart, inner)]
+
+    def slab(cut):
+        low, high = cut
+        at = group()
+        for dy in (1, -1):
+            sy, ty = y_spans(dy, 3)
+            remote(vel_in.at[:, low:high, sy], W.at[:, OFF + low : OFF + high, ty], 0, dy, at)
+        return at
+
+    w_copies = group()
+    for dx, dy in corners:
+        send(w_copies, vel_in, W, 0, OFF, 2, dx, dy, True)
+    for dx in (1, -1):
+        send(w_copies, vel_in, W, 0, OFF, 3, dx, 0, True)
+    slabs = [slab(cut) for cut in cuts[:2]]
     shape = (own_y, own_y)
     diagonal = lax.broadcasted_iota(jnp.int32, shape, 0) == lax.broadcasted_iota(jnp.int32, shape, 1)
     lane16 = lane_of(own_y, nz)
@@ -153,7 +177,14 @@
         column = jnp.sum(jnp.where(diagonal, ground[x : x + 1, :], 0.0), axis=1, keepdims=True)
         low = jnp.where(lane16 == 0, column, 0.0)
         D[OFF + x, 0:own_y, :] = 2.0 * turb[x].astype(F32) + low
-    d_copies = [send(D, D, OFF, OFF, 1, dx, dy) for dx, dy in faces]
+    slabs += [slab(cut) for cut in cuts[2:-1]]
+    d_copies = group()
+    for dx, dy in faces:
+        send(d_copies, D, D, OFF, OFF, 1, dx, dy)
+    slabs += [slab(cut) for cut in cuts[-1:]]
+    p_copies = group()
+    for dx, dy in faces:
+        send(p_copies, pre_in, PA, 0, OFF, 1, dx, dy)
     blank = jnp.zeros((side, nz), F32)
     for r in (1, 2, rows - 3, rows - 2):
         Z[r] = blank
@@ -162,14 +193,13 @@
     blank1 = jnp.zeros((2 * y1, nz), F32)
     for r in (1, 2, half + 5, half + 6):
         H1[r] = blank1
-    for r in (0, 1, half + 6, half + 7):
+    for r in (0, 1, 2, half + 7, half + 8, half + 9):
         H1A[r] = blank1
-    for r in (0, half + 7):
-        H1B[r] = blank1
     loads[3].wait()
     loads[4].wait()
+    hear(0)
+    tell(1)
     finish(w_copies)
-    tell(0)
     lane = lane_of(side, nz)
     first, last = lane == 0, lane == nz - 1
 
@@ -194,27 +224,39 @@
         ghost = 0.03 * jnp.sqrt(2.0 * v[2] * v[2] + flat)
         ghosts = [ghost * v[0], ghost * v[1], (ghost + ghost) * v[2]]
         out = [(T, (0, r), t00), (T, (1, r), t01), (T, (2, r), t02)]
-        drag = D[r] * jnp.sqrt(flat)
         for a, (ty, tz) in enumerate(((t01, t02), (t11, t12), (t12, t22))):
             change = 0.5 * (roll(ty, -1, 0) - roll(ty, 1, 0))
             change += jnp.where(last, -ghosts[a], roll(tz, -1, 1)) - jnp.where(first, ghosts[a], roll(tz, 1, 1))
             change -= v[0] * gx[a] + v[1] * gy[a] + v[2] * gz[a]
-            if a < 2:
-                change -= drag * v[a]
             if a == 0:
                 change += 1.0
             out.append((S, (a, r), v[a] + STEP * change))
         return out
 
+    there = set(range(OFF)) | set(range(OFF + own_x, rows))
+    waiting = list(range(1, rows - 1))
+    for at, (cut, copies) in enumerate(zip(cuts, slabs)):
+        finish(copies)
+        if at == 1:
+            hear(1)
+            tell(2)
+        there |= set(range(OFF + cut[0], OFF + cut[1]))
+        ready = [r for r in waiting if {r - 1, r, r + 1} <= there]
+        waiting = [r for r in waiting if r not in ready]
+        for low in [r for r in ready if r - 1 not in ready]:
+            high = low
+            while high in ready:
+                high += 1
+            loop(low, high, stress_row, G_STRESS)
     finish(d_copies)
-    loop(1, rows - 1, stress_row, G_STRESS)
-    hear(0)
-    tell(1)
 
     def star_row(r):
-        return [
-            (S, (a, r), S[a, r] + (0.5 * STEP) * (T[a, r + 1] - T[a, r - 1])) for a in range(3)
-        ]
+        drag = STEP * (D[r] * jnp.sqrt(W[0, r] * W[0, r] + W[1, r] * W[1, r]))
+        stores = []
+        for a in range(3):
+            v = S[a, r] + (0.5 * STEP) * (T[a, r + 1] - T[a, r - 1])
+            stores.append((S, (a, r), v - drag * W[a, r] if a < 2 else v))
+        return stores
 
     loop(2, rows - 2, star_row, G_FINE)
     finish(p_copies)
@@ -255,11 +297,13 @@
         return [(Z, r, left), (R0, (r + RIM - OFF, slice(0, own_y)), left[0:own_y])]
 
     loop(OFF, OFF + own_x, source_row, G_FINE)
-    r_copies = [send(R0, R0, RIM, RIM, 3, dx, dy) for dx, dy in corners]
-    r_copies += [send(R0, R0, RIM, RIM, RIM, dx, dy) for dx, dy in faces]
+    r_copies = group()
+    for dx, dy in corners:
+        send(r_copies, R0, R0, RIM, RIM, 3, dx, dy)
+    for dx, dy in faces:
+        send(r_copies, R0, R0, RIM, RIM, RIM, dx, dy)
 
     smooth_all(Z, ZA, 2, rows - 2, 1, 1, G_FINE)
-    smooth_all(ZA, ZB, 1, rows - 1, 1, 1, G_FINE)
 
     def pair(v, stride, axis):
         at = lax.broadcasted_iota(jnp.int32, v.shape, axis)
@@ -272,24 +316,52 @@
 
     sub8 = row_of(y1, nz)
 
+    def smooth_pair(src, r, sy, sz):
+        a, b = src[r], src[r + 1]
+        p = a + b
+        lanes = lane_of(p.shape[0], nz)
+        z = jnp.where(lanes >= nz - sz, p, roll(p, -sz, 1)) + jnp.where(lanes < sz, p, roll(p, sz, 1))
+        around = p + src[r - 1] + src[r + 2] + roll(p, -sy, 0) + roll(p, sy, 0) + 4.0 * z
+        return KEEP * p + WEIGHT * around
+
     def fine_residual(i):
-        v = pair(ZB[2 * i + 1] + ZB[2 * i + 2], 1, 1)
+        v = pair(smooth_pair(ZA, 2 * i + 1, 1, 1), 1, 1)
         rim = 0.5 * v[own_y : own_y + 8]
         rim = jnp.where(sub8 == 0, rim + roll(rim, -1, 0), jnp.where(sub8 == 7, rim + roll(rim, 1, 0), 0.0))
         return [(tmp, i, v[0:own_y]), (H1, (i + 3, slice(y1, 2 * y1)), rim)]
 
-    loop(0, half + 2, fine_residual, half + 2)
+    loop(0, half + 2, fine_residual, (half + 2) // 2)
     for i in range(half + 2):
         H1[i + 3, 0:y1] = 0.5 * (tmp[i, pl.ds(0, y1, 2), :] + tmp[i, pl.ds(1, y1, 2), :])
     packs = half // 2
     lane1 = lane_of(2 * y1, nz)
     even1 = lane1 % 2 == 0
+    even = lane_of(y1 + 2, nz) % 2 == 0
+    def put(slot, v):
+        G1[0, slot, 0:y1] = v[0:y1]
+        G1[0, slot, y1 : y1 + 1] = v[y1 : y1 + 1]
+        G1[0, slot, y1 + 1 : y1 + 2] = v[2 * y1 - 1 : 2 * y1]
+
     for i in range(packs):
-        G1[0, 1 + i] = jnp.where(even1, H1[4 + 2 * i], H1[5 + 2 * i])
+        put(1 + i, jnp.where(even1, H1[4 + 2 * i], H1[5 + 2 * i]))
     rim = jnp.where(even1, H1[half + 4], H1[3])
-    G1[0, 0] = rim
-    G1[0, packs + 1] = rim
-    g_copies = []
+    put(0, rim)
+    put(packs + 1, rim)
+    loop(2, half + 6, lambda r: [(H1A, r + 1, smooth(H1, r, 1, 2))], half + 4)
+    lane8 = lane_of(y1, nz)
+    for j in range(quarter + 4):
+        tmp1[j] = pair(smooth_pair(H1A, 2 * j + 1, 1, 2), 2, 1)
+    for which, order in enumerate(((2, 3, 4, 5), (6, 7, 0, 1))):
+        gathered = None
+        for at, j in enumerate(order):
+            v = 0.5 * (tmp1[j, pl.ds(0, y1, 2), :] + tmp1[j, pl.ds(1, y1, 2), :])
+            gathered = v if gathered is None else jnp.where(lane8 % 4 == at, v, gathered)
+        G2[0, REACH, which] = gathered
+    hear(2)
+    h_copies = group()
+    for dx, dy in far:
+        remote(G2.at[0, REACH], G2.at[(ny - dy) % ny, REACH - dx], dx, dy, h_copies)
+    g_copies = group()
     kept = 3
     for dx in (1, -1, 0):
         for dy in range(ny):
@@ -302,22 +374,7 @@
                 src, dst = pl.ds(packs + 1 - kept, kept + 1), pl.ds(packs + 2, kept + 1)
             else:
                 src, dst = pl.ds(0, kept + 1), pl.ds(packs + 3 + kept, kept + 1)
-            g_copies.append(remote(G1.at[0, src], G1.at[k, dst], dx, dy))
-    hear(1)
-    smooth_all(H1, H1A, 2, half + 6, 1, 2)
-    smooth_all(H1A, H1B, 1, half + 7, 1, 2)
-    lane8 = lane_of(y1, nz)
-    for j in range(quarter + 4):
-        tmp1[j] = pair(H1B[2 * j] + H1B[2 * j + 1], 2, 1)
-    for which, order in enumerate(((2, 3, 4, 5), (6, 7, 0, 1))):
-        gathered = None
-        for at, j in enumerate(order):
-            v = 0.5 * (tmp1[j, pl.ds(0, y1, 2), :] + tmp1[j, pl.ds(1, y1, 2), :])
-            gathered = v if gathered is None else jnp.where(lane8 % 4 == at, v, gathered)
-        G2[0, REACH, which] = gathered
-    h_copies = [
-        remote(G2.at[0, REACH], G2.at[(ny - dy) % ny, REACH - dx], dx, dy) for dx, dy in far
-    ]
+            remote(G1.at[0, src], G1.at[k, dst], dx, dy, g_copies)
     finish(r_copies)
     wide = own_x + 2 * RIM
     smooth_all(R0, X1, 1, wide - 1, 1, 1, G_FINE)
@@ -328,36 +385,6 @@
         return [(A, r - 3, PA[r - RIM + OFF] - WEIGHT * total)]
 
     loop(3, wide - 3, base_row, G_FINE)
-    finish(g_copies)
-    full1 = ny * y1
-    count1 = packs + 2 * kept
-
-    def joined(k, q):
-        if q < 0:
-            v = G1[k, packs + 2 + q + kept]
-            return v + jnp.where(even1, 0.0, G1[k, 0]) if q == -1 else v
-        if q >= packs:
-            v = G1[k, packs + 4 + kept + q - packs]
-            return v + jnp.where(even1, G1[k, 0], 0.0) if q == packs else v
-        v = G1[k, 1 + q]
-        if q == 0:
-            v = v + jnp.where(even1, G1[k, packs + 2 + kept], 0.0)
-        if q == packs - 1:
-            v = v + jnp.where(even1, 0.0, G1[k, packs + 3 + kept])
-        return v
-
-    for q in range(-kept, packs + kept):
-        frames = [joined(k, q) for k in range(ny)]
-        for k in range(ny):
-            before, after = frames[(k - 1) % ny][y1:], frames[(k + 1) % ny][y1:]
-            edge = before if ny == 2 else jnp.where(sub8 < y1 // 2, before, after)
-            v = frames[k][0:y1] + edge
-            for bit in (0, 1):
-                f = spread(v, 1, bit)
-                r = 2 * (q + kept) + bit
-                F1[r, k * y1 : (k + 1) * y1, :] = f
-                P1A[r, k * y1 : (k + 1) * y1, :] = -WEIGHT * f
-    sweep(P1A, P1B, F1, 1, 2 * count1 - 1, 1, 2)
     finish(h_copies)
     full2 = ny * y2
     low2 = lane8 % 4 < 2
@@ -404,6 +431,36 @@
         return [(P2B, x, P2B[x] + v) for x in (2 * r, 2 * r + 1)]
 
     loop(6, 12, line_row, 6)
+    finish(g_copies)
+    full1 = ny * y1
+    count1 = packs + 2 * kept
+
+    def joined(k, q):
+        if q < 0:
+            v = G1[k, packs + 2 + q + kept]
+            return v + jnp.where(even, 0.0, G1[k, 0]) if q == -1 else v
+        if q >= packs:
+            v = G1[k, packs + 4 + kept + q - packs]
+            return v + jnp.where(even, G1[k, 0], 0.0) if q == packs else v
+        v = G1[k, 1 + q]
+        if q == 0:
+            v = v + jnp.where(even, G1[k, packs + 2 + kept], 0.0)
+        if q == packs - 1:
+            v = v + jnp.where(even, 0.0, G1[k, packs + 3 + kept])
+        return v
+
+    for q in range(-kept, packs + kept):
+        frames = [joined(k, q) for k in range(ny)]
+        for k in range(ny):
+            before, after = frames[(k - 1) % ny], frames[(k + 1) % ny]
+            v = frames[k][0:y1] + jnp.where(sub8 == 0, before[y1 : y1 + 1], 0.0)
+            v = v + jnp.where(sub8 == y1 - 1, after[y1 + 1 : y1 + 2], 0.0)
+            for bit in (0, 1):
+                f = spread(v, 1, bit)
+                r = 2 * (q + kept) + bit
+                F1[r, k * y1 : (k + 1) * y1, :] = f
+                P1A[r, k * y1 : (k + 1) * y1, :] = -WEIGHT * f
+    sweep(P1A, P1B, F1, 1, 2 * count1 - 1, 1, 2)
     sweep(P2B, P2A, F2, 13, 23, 1, 4)
 
     def second_row(m):
@@ -438,13 +495,13 @@
 
     loop(1, 11, first_pair, 5)
     loop(1, own_x + 3, lambda r: [(PN, r - 1, A[r - 1] + smooth(Y1, r, 1, 1))], 6)
+    await_lines(send_sem.at[0], sum(sent))
 
 
 def closing(S, PN, vel_out, pre_out, vel, pre, sem):
     _, own_x, own_y, nz = vel.shape
     lane = lane_of(PN.shape[1], nz)
     first, last = lane == 0, lane == nz - 1
-    copies = []
     part = 4
     for low in range(0, own_x, part):
         for x in range(low, low + part):
@@ -456,13 +513,10 @@
             for a, g in enumerate((gx, gy, gz)):
                 vel[a, x] = S[a, OFF + x, 0:own_y] - g[0:own_y]
         span = pl.ds(low, part)
-        at = len(copies)
-        copies.append(pltpu.make_async_copy(vel.at[:, span], vel_out.at[:, span], sem.at[at]))
-        copies.append(pltpu.make_async_copy(pre.at[span], pre_out.at[span], sem.at[at + 1]))
-        copies[-2].start()
-        copies[-1].start()
-    for copy in copies:
-        copy.wait()
+        pltpu.make_async_copy(vel.at[:, span], vel_out.at[:, span], sem.at[0]).start()
+        pltpu.make_async_copy(pre.at[span], pre_out.at[span], sem.at[1]).start()
+    pltpu.make_async_copy(vel, vel_out, sem.at[0]).wait()
+    pltpu.make_async_copy(pre, pre_out, sem.at[1]).wait()
 
 
 def per_device(nx, ny, velocity, pressure, land_type, turbine_cells, surface_drag):
@@ -483,25 +537,28 @@
     level2 = window(rows2, full2)
     level3 = window(rows2 // 2, full2)
     frame1 = window(half + 8, 2 * y1)
-    count = 8 + 4 + 4 + 8 + 3 * ny - 1 + (2 * REACH + 1) * ny - 1
+    corner, face = 4 * (3 * 2 * 2 + 3 * 3), 2 * (own_x + own_y)
+    total = corner + face * (3 * 3 + 1 + 1 + RIM)
+    total += 5 * (y1 + 2) * 3 * ny + (2 * REACH + 1) * ny * 2 * y1
     scratch = [
         window(3, rows, side), window(rows, side), window(rows, side), window(rows, side),
         window(3, rows, side), window(wide, side),
-        window(rows, side), window(rows, side), window(rows, side),
+        window(rows, side), window(rows, side),
         window(wide, side), window(wide, side), window(own_x + 2, side), window(own_x + 4, side),
         window(half + 2, own_y), window(quarter + 4, 2 * y1),
         pltpu.VMEM((own_x, own_y, nz), jnp.int32),
         pltpu.VMEM(land_type.shape, jnp.int32),
         pltpu.SMEM(surface_drag.shape, F32),
-        frame1, frame1, frame1, window(ny, packs + 10, 2 * y1),
+        frame1, window(half + 10, 2 * y1), window(ny, packs + 10, y1 + 2),
         level1, level1, level1,
         window(ny, 2 * REACH + 1, 2, y1),
         level2, level2, level2, level3, level3, level3,
         window(8, full1), window(12, side),
+        window(total),
         pltpu.SemaphoreType.DMA((5,)),
-        pltpu.SemaphoreType.DMA((count,)),
-        pltpu.SemaphoreType.DMA((count,)),
-        pltpu.SemaphoreType.REGULAR((2, 2)),
+        pltpu.SemaphoreType.DMA((1,)),
+        pltpu.SemaphoreType.DMA((11,)),
+        pltpu.SemaphoreType.REGULAR((3,)),
     ]
     inside = pl.BlockSpec(memory_space=pltpu.VMEM)
     outside = pl.BlockSpec(memory_space=pltpu.HBM)
@@ -533,7 +590,7 @@
         scratch_shapes=[
             pltpu.VMEM(velocity.shape, F32),
             pltpu.VMEM(pressure.shape, F32),
-            pltpu.SemaphoreType.DMA((2 * own_x // 4,)),
+            pltpu.SemaphoreType.DMA((2,)),
         ],
         compiler_params=pltpu.CompilerParams(vmem_limit_bytes=VMEM_LIMIT),
     )(star, middle)

time: 25.2 us -> 23 us (0.913)
  Pallas kernels: 24.4 us -> 22.2 us
    pallas_call x1, Pallas kernels: 23.5 us -> 21.3 us  [per_device(): pl.pallas_call(functools.partial(kernel, nx, ny), out_shape=(jax.ShapeDty...]
where the time goes in v2:
time: 23 us; the launch traced here: 22.9 us
  Pallas kernels  22.2 us (97%)
  between operations  0.64 us (3%)
    pallas_call x1, Pallas kernels, per_device(): pl.pallas_call(functools.partial(kernel, nx, ny), out_shape=(jax.ShapeDty...  21.3 us
    pallas_call x1, Pallas kernels, per_device(): pl.pallas_call(closing, out_shape=(jax.ShapeDtypeStruct(velocity.shape, F...  0.88 us

profile of v2, /device:TPU:0, one launch (start us, length us, event | category | flops | bytes accessed | tf_op | source)
XLA Modules:
  0.0 22.9 jit_solution(5423984491502487847)
XLA Ops:
  0.6 21.3 %shard_map.68 = (f32[3,22,24,128]{3,2,1,0:T(8,128)S(1)}, f32[18,24,128]{2,1,0:T(8,128)S(1)}) custom-call(f32[3,16,16,128]{3,2,1,0:T(8,128)} %vel_in.1, f32[16,16,128]{2,1,0:T(8,128)} %pre_in.1, s32[16,16,128]{2,1,0:T(8,128)} %turb_in.1, s32[16,16]{1,0:T(8,128)} %land_in.1, f32[16]{0:T(128)} %coeff_in.1), custom_call_target="tpu_custom_call" | custom-call | tf_op jit(solution)/shard_map/pallas_call | solution.py:569
  22.0 0.9 %shard_map.69 = (f32[3,16,16,128]{3,2,1,0:T(8,128)}, f32[16,16,128]{2,1,0:T(8,128)}) custom-call(f32[3,22,24,128]{3,2,1,0:T(8,128)S(1)} %get-tuple-element.4.S, f32[18,24,128]{2,1,0:T(8,128)S(1)} %get-tuple-element.5.PN), custom_call_target="tpu_custom_call" | custom-call | tf_op jit(solution)/shard_map/pallas_call | solution.py:582

commit v3 on v2

--- a/solution.py
+++ b/solution.py
@@ -56,7 +56,7 @@
 def kernel(
     nx, ny, vel_in, pre_in, turb_in, land_in, coeff_in, S, PN,
     W, D, PA, F, T, R0, Z, ZA, X1, X2, A, Y1, tmp, tmp1, turb, land, coeff,
-    H1, H1A, G1, F1, P1A, P1B, G2, F2, P2A, P2B, F3, P3A, P3B, E1, E0,
+    H1, H1A, G1, F1, P1A, P1B, G2, GX, F2, P2A, P2B, F3, P3A, P3B, E1, E0,
     spare, load_sem, send_sem, recv_sem, token,
 ):
     me_x, me_y = lax.axis_index("gx"), lax.axis_index("gy")
@@ -144,10 +144,10 @@
 
     pl.semaphore_wait(barrier, len(close))
     tell(0)
-    quart = own_x // 4
-    inner = (own_x - 2 * quart + 2) // 3
-    cuts = [(0, quart), (own_x - quart, own_x)]
-    cuts += [(low, min(low + inner, own_x - quart)) for low in range(quart, own_x - quart, inner)]
+    piece = own_x // 4
+    low_end, high_end = 2 * piece, own_x - own_x // 8
+    middle = (low_end + high_end) // 2
+    cuts = [(0, piece), (piece, low_end), (low_end, middle), (middle, high_end), (high_end, own_x)]
 
     def slab(cut):
         low, high = cut
@@ -177,14 +177,13 @@
         column = jnp.sum(jnp.where(diagonal, ground[x : x + 1, :], 0.0), axis=1, keepdims=True)
         low = jnp.where(lane16 == 0, column, 0.0)
         D[OFF + x, 0:own_y, :] = 2.0 * turb[x].astype(F32) + low
-    slabs += [slab(cut) for cut in cuts[2:-1]]
     d_copies = group()
     for dx, dy in faces:
         send(d_copies, D, D, OFF, OFF, 1, dx, dy)
-    slabs += [slab(cut) for cut in cuts[-1:]]
     p_copies = group()
     for dx, dy in faces:
         send(p_copies, pre_in, PA, 0, OFF, 1, dx, dy)
+    slabs += [slab(cut) for cut in cuts[2:]]
     blank = jnp.zeros((side, nz), F32)
     for r in (1, 2, rows - 3, rows - 2):
         Z[r] = blank
@@ -199,7 +198,6 @@
     loads[4].wait()
     hear(0)
     tell(1)
-    finish(w_copies)
     lane = lane_of(side, nz)
     first, last = lane == 0, lane == nz - 1
 
@@ -233,23 +231,6 @@
             out.append((S, (a, r), v[a] + STEP * change))
         return out
 
-    there = set(range(OFF)) | set(range(OFF + own_x, rows))
-    waiting = list(range(1, rows - 1))
-    for at, (cut, copies) in enumerate(zip(cuts, slabs)):
-        finish(copies)
-        if at == 1:
-            hear(1)
-            tell(2)
-        there |= set(range(OFF + cut[0], OFF + cut[1]))
-        ready = [r for r in waiting if {r - 1, r, r + 1} <= there]
-        waiting = [r for r in waiting if r not in ready]
-        for low in [r for r in ready if r - 1 not in ready]:
-            high = low
-            while high in ready:
-                high += 1
-            loop(low, high, stress_row, G_STRESS)
-    finish(d_copies)
-
     def star_row(r):
         drag = STEP * (D[r] * jnp.sqrt(W[0, r] * W[0, r] + W[1, r] * W[1, r]))
         stores = []
@@ -258,8 +239,6 @@
             stores.append((S, (a, r), v - drag * W[a, r] if a < 2 else v))
         return stores
 
-    loop(2, rows - 2, star_row, G_FINE)
-    finish(p_copies)
 
     def stencil(src, r, sy, sz):
         p = src[r]
@@ -296,15 +275,6 @@
         left = jnp.where(own, f - (around - 12.0 * p), 0.0)
         return [(Z, r, left), (R0, (r + RIM - OFF, slice(0, own_y)), left[0:own_y])]
 
-    loop(OFF, OFF + own_x, source_row, G_FINE)
-    r_copies = group()
-    for dx, dy in corners:
-        send(r_copies, R0, R0, RIM, RIM, 3, dx, dy)
-    for dx, dy in faces:
-        send(r_copies, R0, R0, RIM, RIM, RIM, dx, dy)
-
-    smooth_all(Z, ZA, 2, rows - 2, 1, 1, G_FINE)
-
     def pair(v, stride, axis):
         at = lax.broadcasted_iota(jnp.int32, v.shape, axis)
         even = (at // stride) % 2 == 0
@@ -330,9 +300,73 @@
         rim = jnp.where(sub8 == 0, rim + roll(rim, -1, 0), jnp.where(sub8 == 7, rim + roll(rim, 1, 0), 0.0))
         return [(tmp, i, v[0:own_y]), (H1, (i + 3, slice(y1, 2 * y1)), rim)]
 
-    loop(0, half + 2, fine_residual, (half + 2) // 2)
-    for i in range(half + 2):
-        H1[i + 3, 0:y1] = 0.5 * (tmp[i, pl.ds(0, y1, 2), :] + tmp[i, pl.ds(1, y1, 2), :])
+
+    def coarsen_row(i):
+        return [(H1, (i + 3, slice(0, y1)), 0.5 * (tmp[i, pl.ds(0, y1, 2), :] + tmp[i, pl.ds(1, y1, 2), :]))]
+
+    here = set()
+    late = set(range(2, rows - 2))
+    zero = {0, 1, 2, rows - 3, rows - 2, rows - 1}
+    done = {name: set() for name in ("stress", "star", "source", "smooth", "pair", "coarsen")}
+
+    def around_of(r):
+        return {r - 1, r, r + 1}
+
+    def run(name, rows_of, ready, body, size):
+        fresh = [r for r in rows_of if r not in done[name] and ready(r)]
+        for low in [r for r in fresh if r - 1 not in fresh]:
+            high = low
+            while high in fresh:
+                high += 1
+            loop(low, high, body, min(size, high - low))
+        done[name] |= set(fresh)
+
+    def advance(sides):
+        run("stress", range(1, rows - 1), lambda r: around_of(r) <= here, stress_row, G_STRESS)
+        if not sides:
+            return
+        run("star", range(2, rows - 2), lambda r: around_of(r) <= done["stress"], star_row, G_FINE)
+        run("source", range(OFF, OFF + own_x), lambda r: around_of(r) <= done["star"], source_row, G_FINE)
+        known = done["source"] | zero
+        run("smooth", range(2, rows - 2), lambda r: around_of(r) <= known,
+            lambda r: [(ZA, r, smooth(Z, r, 1, 1))], G_FINE)
+        known1 = done["smooth"] | {0, 1, rows - 2, rows - 1}
+        run("pair", range(half + 2), lambda i: set(range(2 * i, 2 * i + 4)) <= known1, fine_residual, 5)
+        run("coarsen", range(half + 2), lambda i: i in done["pair"], coarsen_row, half + 2)
+
+    def r0_faces(low, high):
+        for dy in (1, -1):
+            sy, ty = y_spans(dy, RIM)
+            span = slice(low - OFF + RIM, high - OFF + RIM)
+            remote(R0.at[span, sy], R0.at[span, ty], 0, dy, r_copies)
+
+    def r0_side(dx):
+        for dy in (1, -1):
+            send(r_copies, R0, R0, RIM, RIM, 3, dx, dy)
+        send(r_copies, R0, R0, RIM, RIM, RIM, dx, 0)
+
+    r_copies = group()
+    for at, (cut, copies) in enumerate(zip(cuts, slabs)):
+        with jax.named_scope("SL%d" % at): finish(copies)
+        here |= set(range(OFF + cut[0], OFF + cut[1]))
+        with jax.named_scope("ST%d" % at): advance(at > 3)
+        if at == 1:
+            hear(1)
+            tell(2)
+        if at == 3:
+            with jax.named_scope("WX"):
+                finish(d_copies)
+                finish(p_copies)
+                finish(w_copies)
+            here |= set(range(OFF)) | set(range(OFF + own_x, rows))
+            with jax.named_scope("SX"): advance(True)
+            split = OFF
+            while split in done["source"]:
+                split += 1
+            r0_faces(OFF, split)
+            r0_side(-1)
+    r0_faces(split, OFF + own_x)
+    r0_side(1)
     packs = half // 2
     lane1 = lane_of(2 * y1, nz)
     even1 = lane1 % 2 == 0
@@ -357,10 +391,21 @@
             v = 0.5 * (tmp1[j, pl.ds(0, y1, 2), :] + tmp1[j, pl.ds(1, y1, 2), :])
             gathered = v if gathered is None else jnp.where(lane8 % 4 == at, v, gathered)
         G2[0, REACH, which] = gathered
-    hear(2)
+    low2 = lane8 % 4 < 2
+    near, beyond = G2[0, REACH, 0], G2[0, REACH, 1]
+    GX[0] = jnp.where(low2, beyond, near)
+    GX[1] = jnp.where(low2, near, beyond)
     h_copies = group()
-    for dx, dy in far:
-        remote(G2.at[0, REACH], G2.at[(ny - dy) % ny, REACH - dx], dx, dy, h_copies)
+    for distance in [3, 2, 4, 1, 0]:
+        if distance == REACH:
+            hear(2)
+        for dx, dy in far:
+            if abs(dx) == distance:
+                slot = G2.at[(ny - dy) % ny, REACH - dx]
+                if distance == REACH:
+                    remote(GX.at[0 if dx > 0 else 1], slot.at[0], dx, dy, h_copies)
+                else:
+                    remote(G2.at[0, REACH], slot, dx, dy, h_copies)
     g_copies = group()
     kept = 3
     for dx in (1, -1, 0):
@@ -387,12 +432,15 @@
     loop(3, wide - 3, base_row, G_FINE)
     finish(h_copies)
     full2 = ny * y2
-    low2 = lane8 % 4 < 2
     blank8 = jnp.zeros((y1, nz), F32)
+    ends = (0, 2 * REACH)
+
+    def spill(k, s):
+        return G2[k, s, 0 if s in ends else 1]
 
     def joined2(k, s):
-        before = G2[k, s - 1, 1] if s > 0 else blank8
-        after = G2[k, s + 1, 1] if s < 2 * REACH else blank8
+        before = spill(k, s - 1) if s > 0 else blank8
+        after = spill(k, s + 1) if s < 2 * REACH else blank8
         return G2[k, s, 0] + jnp.where(low2, before, after)
 
     for s in range(2 * REACH + 1):
@@ -551,7 +599,7 @@
         pltpu.SMEM(surface_drag.shape, F32),
         frame1, window(half + 10, 2 * y1), window(ny, packs + 10, y1 + 2),
         level1, level1, level1,
-        window(ny, 2 * REACH + 1, 2, y1),
+        window(ny, 2 * REACH + 1, 2, y1), window(2, y1),
         level2, level2, level2, level3, level3, level3,
         window(8, full1), window(12, side),
         window(total),

time: 23 us -> 22.3 us (0.970)
  Pallas kernels: 22.2 us -> 21.5 us
    pallas_call x1, Pallas kernels: 21.3 us -> 20.6 us  [per_device(): pl.pallas_call(functools.partial(kernel, nx, ny), out_shape=(jax.ShapeDty...]
where the time goes in v3:
time: 22.3 us; the launch traced here: 22.1 us
  Pallas kernels  21.5 us (96%)
  between operations  0.64 us (3%)
    pallas_call x1, Pallas kernels, per_device(): pl.pallas_call(functools.partial(kernel, nx, ny), out_shape=(jax.ShapeDty...  20.6 us
    pallas_call x1, Pallas kernels, per_device(): pl.pallas_call(closing, out_shape=(jax.ShapeDtypeStruct(velocity.shape, F...  0.88 us

profile of v3, /device:TPU:0, one launch (start us, length us, event | category | flops | bytes accessed | tf_op | source)
XLA Modules:
  0.0 22.1 jit_solution(1083903902929099833)
XLA Ops:
  0.6 20.6 %shard_map.68 = (f32[3,22,24,128]{3,2,1,0:T(8,128)S(1)}, f32[18,24,128]{2,1,0:T(8,128)S(1)}) custom-call(f32[3,16,16,128]{3,2,1,0:T(8,128)} %vel_in.1, f32[16,16,128]{2,1,0:T(8,128)} %pre_in.1, s32[16,16,128]{2,1,0:T(8,128)} %turb_in.1, s32[16,16]{1,0:T(8,128)} %land_in.1, f32[16]{0:T(128)} %coeff_in.1), custom_call_target="tpu_custom_call" | custom-call | tf_op jit(solution)/shard_map/pallas_call | solution.py:617
  21.3 0.9 %shard_map.69 = (f32[3,16,16,128]{3,2,1,0:T(8,128)}, f32[16,16,128]{2,1,0:T(8,128)}) custom-call(f32[3,22,24,128]{3,2,1,0:T(8,128)S(1)} %get-tuple-element.4.S, f32[18,24,128]{2,1,0:T(8,128)S(1)} %get-tuple-element.5.PN), custom_call_target="tpu_custom_call" | custom-call | tf_op jit(solution)/shard_map/pallas_call | solution.py:630

commit v4 on v3

--- a/solution.py
+++ b/solution.py
@@ -135,15 +135,26 @@
     corners = [(dx, dy) for dx in (1, -1) for dy in (1, -1)]
     faces = [(0, 1), (0, -1), (1, 0), (-1, 0)]
 
-    def tell(turn):
-        for dx in (1, -1):
-            pl.semaphore_signal(token.at[turn], inc=1, device_id=device(dx, 0), device_id_type=MESH)
-
-    def hear(turn):
-        pl.semaphore_wait(token.at[turn], 2)
+    def hear(turn, dx):
+        at = turn + (0 if dx < 0 else 3)
+        pl.semaphore_wait(token.at[at], 1)
+        if turn < 2:
+            tell(turn + 1, -dx)
+
+    def tell(turn, dx):
+        at = turn + (3 if dx < 0 else 0)
+        pl.semaphore_signal(token.at[at], inc=1, device_id=device(dx, 0), device_id_type=MESH)
+
+    def hear_right(turn, crosses):
+        end = me_x >= nx - 1 - turn
+
+        @pl.when(end if crosses else jnp.logical_not(end))
+        def _():
+            hear(turn, 1)
 
     pl.semaphore_wait(barrier, len(close))
-    tell(0)
+    tell(0, 1)
+    tell(0, -1)
     piece = own_x // 4
     low_end, high_end = 2 * piece, own_x - own_x // 8
     middle = (low_end + high_end) // 2
@@ -157,11 +168,11 @@
             remote(vel_in.at[:, low:high, sy], W.at[:, OFF + low : OFF + high, ty], 0, dy, at)
         return at
 
-    w_copies = group()
-    for dx, dy in corners:
-        send(w_copies, vel_in, W, 0, OFF, 2, dx, dy, True)
-    for dx in (1, -1):
-        send(w_copies, vel_in, W, 0, OFF, 3, dx, 0, True)
+    low_copies, high_copies = group(), group()
+    for dx, at in ((-1, high_copies), (1, low_copies)):
+        for dy in (1, -1):
+            send(at, vel_in, W, 0, OFF, 2, dx, dy, True)
+        send(at, vel_in, W, 0, OFF, 3, dx, 0, True)
     slabs = [slab(cut) for cut in cuts[:2]]
     shape = (own_y, own_y)
     diagonal = lax.broadcasted_iota(jnp.int32, shape, 0) == lax.broadcasted_iota(jnp.int32, shape, 1)
@@ -179,10 +190,9 @@
         D[OFF + x, 0:own_y, :] = 2.0 * turb[x].astype(F32) + low
     d_copies = group()
     for dx, dy in faces:
-        send(d_copies, D, D, OFF, OFF, 1, dx, dy)
-    p_copies = group()
-    for dx, dy in faces:
-        send(p_copies, pre_in, PA, 0, OFF, 1, dx, dy)
+        at = high_copies if dx == -1 else d_copies
+        send(at, D, D, OFF, OFF, 1, dx, dy)
+        send(at, pre_in, PA, 0, OFF, 1, dx, dy)
     slabs += [slab(cut) for cut in cuts[2:]]
     blank = jnp.zeros((side, nz), F32)
     for r in (1, 2, rows - 3, rows - 2):
@@ -196,8 +206,6 @@
         H1A[r] = blank1
     loads[3].wait()
     loads[4].wait()
-    hear(0)
-    tell(1)
     lane = lane_of(side, nz)
     first, last = lane == 0, lane == nz - 1
 
@@ -304,8 +312,7 @@
     def coarsen_row(i):
         return [(H1, (i + 3, slice(0, y1)), 0.5 * (tmp[i, pl.ds(0, y1, 2), :] + tmp[i, pl.ds(1, y1, 2), :]))]
 
-    here = set()
-    late = set(range(2, rows - 2))
+    here, behind = set(), set()
     zero = {0, 1, 2, rows - 3, rows - 2, rows - 1}
     done = {name: set() for name in ("stress", "star", "source", "smooth", "pair", "coarsen")}
 
@@ -321,12 +328,12 @@
             loop(low, high, body, min(size, high - low))
         done[name] |= set(fresh)
 
-    def advance(sides):
+    def advance(full):
         run("stress", range(1, rows - 1), lambda r: around_of(r) <= here, stress_row, G_STRESS)
-        if not sides:
+        if not full:
             return
-        run("star", range(2, rows - 2), lambda r: around_of(r) <= done["stress"], star_row, G_FINE)
-        run("source", range(OFF, OFF + own_x), lambda r: around_of(r) <= done["star"], source_row, G_FINE)
+        run("star", range(2, rows - 2), lambda r: around_of(r) <= done["stress"] and r in behind, star_row, G_FINE)
+        run("source", range(OFF, OFF + own_x), lambda r: around_of(r) <= done["star"] & behind, source_row, G_FINE)
         known = done["source"] | zero
         run("smooth", range(2, rows - 2), lambda r: around_of(r) <= known,
             lambda r: [(ZA, r, smooth(Z, r, 1, 1))], G_FINE)
@@ -346,25 +353,35 @@
         send(r_copies, R0, R0, RIM, RIM, RIM, dx, 0)
 
     r_copies = group()
-    for at, (cut, copies) in enumerate(zip(cuts, slabs)):
-        with jax.named_scope("SL%d" % at): finish(copies)
-        here |= set(range(OFF + cut[0], OFF + cut[1]))
-        with jax.named_scope("ST%d" % at): advance(at > 3)
-        if at == 1:
-            hear(1)
-            tell(2)
-        if at == 3:
-            with jax.named_scope("WX"):
-                finish(d_copies)
-                finish(p_copies)
-                finish(w_copies)
-            here |= set(range(OFF)) | set(range(OFF + own_x, rows))
-            with jax.named_scope("SX"): advance(True)
-            split = OFF
-            while split in done["source"]:
-                split += 1
-            r0_faces(OFF, split)
-            r0_side(-1)
+    split = OFF
+
+    def arrive(copies, low, high, full):
+        finish(copies)
+        here.update(range(OFF + low, OFF + high))
+        advance(full)
+
+    for turn in range(3):
+        hear_right(turn, False)
+        hear(turn, -1)
+    arrive(slabs[0], *cuts[0], False)
+    arrive(low_copies, -OFF, 0, False)
+    arrive(slabs[1], *cuts[1], False)
+    finish(d_copies)
+    high_rows = set(range(OFF + own_x, rows))
+    behind.update(range(OFF + own_x))
+    advance(True)
+    arrive(slabs[2], *cuts[2], True)
+    arrive(slabs[3], *cuts[3], True)
+    while split in done["source"]:
+        split += 1
+    r0_faces(OFF, split)
+    r0_side(-1)
+    for turn in range(3):
+        hear_right(turn, True)
+    finish(high_copies)
+    here.update(high_rows)
+    behind.update(high_rows)
+    arrive(slabs[4], *cuts[4], True)
     r0_faces(split, OFF + own_x)
     r0_side(1)
     packs = half // 2
@@ -396,16 +413,23 @@
     GX[0] = jnp.where(low2, beyond, near)
     GX[1] = jnp.where(low2, near, beyond)
     h_copies = group()
-    for distance in [3, 2, 4, 1, 0]:
-        if distance == REACH:
-            hear(2)
-        for dx, dy in far:
-            if abs(dx) == distance:
-                slot = G2.at[(ny - dy) % ny, REACH - dx]
-                if distance == REACH:
-                    remote(GX.at[0 if dx > 0 else 1], slot.at[0], dx, dy, h_copies)
-                else:
-                    remote(G2.at[0, REACH], slot, dx, dy, h_copies)
+    order = sorted(far, key=lambda to: (to[0] == 0, abs(to[0]) == 1, -to[0], -to[1]))
+
+    def spread_out(sign):
+        for dx, dy in order:
+            dx = sign * dx
+            slot = G2.at[(ny - dy) % ny, REACH - dx]
+            if abs(dx) == REACH:
+                remote(GX.at[0 if dx > 0 else 1], slot.at[0], dx, dy, h_copies)
+            else:
+                remote(G2.at[0, REACH], slot, dx, dy, h_copies)
+
+    second = me_x >= nx // 2
+    size = groups[h_copies], len(sent)
+    pl.when(second)(lambda: spread_out(1))
+    groups[h_copies] = size[0]
+    del sent[size[1]:]
+    pl.when(jnp.logical_not(second))(lambda: spread_out(-1))
     g_copies = group()
     kept = 3
     for dx in (1, -1, 0):
@@ -606,7 +630,7 @@
         pltpu.SemaphoreType.DMA((5,)),
         pltpu.SemaphoreType.DMA((1,)),
         pltpu.SemaphoreType.DMA((11,)),
-        pltpu.SemaphoreType.REGULAR((3,)),
+        pltpu.SemaphoreType.REGULAR((6,)),
     ]
     inside = pl.BlockSpec(memory_space=pltpu.VMEM)
     outside = pl.BlockSpec(memory_space=pltpu.HBM)

time: 22.3 us -> 21.5 us (0.964)
  Pallas kernels: 21.5 us -> 20.8 us
    pallas_call x1, Pallas kernels: 20.6 us -> 19.9 us  [per_device(): pl.pallas_call(functools.partial(kernel, nx, ny), out_shape=(jax.ShapeDty...]
where the time goes in v4:
time: 21.5 us; the launch traced here: 21.4 us
  Pallas kernels  20.8 us (97%)
  between operations  0.64 us (3%)
    pallas_call x1, Pallas kernels, per_device(): pl.pallas_call(functools.partial(kernel, nx, ny), out_shape=(jax.ShapeDty...  19.9 us
    pallas_call x1, Pallas kernels, per_device(): pl.pallas_call(closing, out_shape=(jax.ShapeDtypeStruct(velocity.shape, F...  0.88 us

profile of v4, /device:TPU:0, one launch (start us, length us, event | category | flops | bytes accessed | tf_op | source)
XLA Modules:
  0.0 21.4 jit_solution(8589596808352841770)
XLA Ops:
  0.6 19.9 %shard_map.68 = (f32[3,22,24,128]{3,2,1,0:T(8,128)S(1)}, f32[18,24,128]{2,1,0:T(8,128)S(1)}) custom-call(f32[3,16,16,128]{3,2,1,0:T(8,128)} %vel_in.1, f32[16,16,128]{2,1,0:T(8,128)} %pre_in.1, s32[16,16,128]{2,1,0:T(8,128)} %turb_in.1, s32[16,16]{1,0:T(8,128)} %land_in.1, f32[16]{0:T(128)} %coeff_in.1), custom_call_target="tpu_custom_call" | custom-call | tf_op jit(solution)/shard_map/pallas_call | solution.py:641
  20.5 0.9 %shard_map.69 = (f32[3,16,16,128]{3,2,1,0:T(8,128)}, f32[16,16,128]{2,1,0:T(8,128)}) custom-call(f32[3,22,24,128]{3,2,1,0:T(8,128)S(1)} %get-tuple-element.4.S, f32[18,24,128]{2,1,0:T(8,128)S(1)} %get-tuple-element.5.PN), custom_call_target="tpu_custom_call" | custom-call | tf_op jit(solution)/shard_map/pallas_call | solution.py:654

commit v5 on v4

--- a/solution.py
+++ b/solution.py
@@ -56,7 +56,7 @@
 def kernel(
     nx, ny, vel_in, pre_in, turb_in, land_in, coeff_in, S, PN,
     W, D, PA, F, T, R0, Z, ZA, X1, X2, A, Y1, tmp, tmp1, turb, land, coeff,
-    H1, H1A, G1, F1, P1A, P1B, G2, GX, F2, P2A, P2B, F3, P3A, P3B, E1, E0,
+    H1, H1A, G1, F1, P1A, P1B, G2, GX, F2, P2A, P2B, F3, P3A, P3B, P3C, E1, E0,
     spare, load_sem, send_sem, recv_sem, token,
 ):
     me_x, me_y = lax.axis_index("gx"), lax.axis_index("gy")
@@ -345,14 +345,15 @@
         for dy in (1, -1):
             sy, ty = y_spans(dy, RIM)
             span = slice(low - OFF + RIM, high - OFF + RIM)
-            remote(R0.at[span, sy], R0.at[span, ty], 0, dy, r_copies)
+            remote(R0.at[span, sy], R0.at[span, ty], 0, dy, face_copies)
 
     def r0_side(dx):
+        at = left_copies if dx == 1 else right_copies
         for dy in (1, -1):
-            send(r_copies, R0, R0, RIM, RIM, 3, dx, dy)
-        send(r_copies, R0, R0, RIM, RIM, RIM, dx, 0)
-
-    r_copies = group()
+            send(at, R0, R0, RIM, RIM, 3, dx, dy)
+        send(at, R0, R0, RIM, RIM, RIM, dx, 0)
+
+    face_copies, left_copies, right_copies = group(), group(), group()
     split = OFF
 
     def arrive(copies, low, high, full):
@@ -370,14 +371,15 @@
     high_rows = set(range(OFF + own_x, rows))
     behind.update(range(OFF + own_x))
     advance(True)
+    hear_right(0, True)
     arrive(slabs[2], *cuts[2], True)
+    hear_right(1, True)
     arrive(slabs[3], *cuts[3], True)
     while split in done["source"]:
         split += 1
     r0_faces(OFF, split)
     r0_side(-1)
-    for turn in range(3):
-        hear_right(turn, True)
+    hear_right(2, True)
     finish(high_copies)
     here.update(high_rows)
     behind.update(high_rows)
@@ -398,6 +400,20 @@
     rim = jnp.where(even1, H1[half + 4], H1[3])
     put(0, rim)
     put(packs + 1, rim)
+    g_copies = group()
+    kept = 3
+    for dx in (1, -1, 0):
+        for dy in range(ny):
+            if dx == 0 and dy == 0:
+                continue
+            k = (ny - dy) % ny
+            if dx == 0:
+                src, dst = pl.ds(0, packs + 1), pl.ds(0, packs + 1)
+            elif dx == 1:
+                src, dst = pl.ds(packs + 1 - kept, kept + 1), pl.ds(packs + 2, kept + 1)
+            else:
+                src, dst = pl.ds(0, kept + 1), pl.ds(packs + 3 + kept, kept + 1)
+            remote(G1.at[0, src], G1.at[k, dst], dx, dy, g_copies)
     loop(2, half + 6, lambda r: [(H1A, r + 1, smooth(H1, r, 1, 2))], half + 4)
     lane8 = lane_of(y1, nz)
     for j in range(quarter + 4):
@@ -430,79 +446,27 @@
     groups[h_copies] = size[0]
     del sent[size[1]:]
     pl.when(jnp.logical_not(second))(lambda: spread_out(-1))
-    g_copies = group()
-    kept = 3
-    for dx in (1, -1, 0):
-        for dy in range(ny):
-            if dx == 0 and dy == 0:
-                continue
-            k = (ny - dy) % ny
-            if dx == 0:
-                src, dst = pl.ds(0, packs + 1), pl.ds(0, packs + 1)
-            elif dx == 1:
-                src, dst = pl.ds(packs + 1 - kept, kept + 1), pl.ds(packs + 2, kept + 1)
-            else:
-                src, dst = pl.ds(0, kept + 1), pl.ds(packs + 3 + kept, kept + 1)
-            remote(G1.at[0, src], G1.at[k, dst], dx, dy, g_copies)
-    finish(r_copies)
     wide = own_x + 2 * RIM
-    smooth_all(R0, X1, 1, wide - 1, 1, 1, G_FINE)
-    smooth_all(X1, X2, 2, wide - 2, 1, 1, G_FINE)
 
     def base_row(r):
         total = R0[r] + X1[r] + X2[r] + smooth(X2, r, 1, 1)
         return [(A, r - 3, PA[r - RIM + OFF] - WEIGHT * total)]
 
-    loop(3, wide - 3, base_row, G_FINE)
-    finish(h_copies)
-    full2 = ny * y2
-    blank8 = jnp.zeros((y1, nz), F32)
-    ends = (0, 2 * REACH)
-
-    def spill(k, s):
-        return G2[k, s, 0 if s in ends else 1]
-
-    def joined2(k, s):
-        before = spill(k, s - 1) if s > 0 else blank8
-        after = spill(k, s + 1) if s < 2 * REACH else blank8
-        return G2[k, s, 0] + jnp.where(low2, before, after)
-
-    for s in range(2 * REACH + 1):
-        frames = [joined2(k, s) for k in range(ny)]
-        turned = [roll(v, y2, 0) for v in frames]
-        for m in range(ny // 2):
-            k = 2 * m
-            if ny == 2:
-                v = frames[0] + turned[1]
-            else:
-                lower = frames[k] + jnp.where(sub8 < 2, turned[(k - 1) % ny], turned[(k + 1) % ny])
-                upper = turned[k + 1] + jnp.where(sub8 < 6, frames[k], frames[(k + 2) % ny])
-                v = jnp.where(sub8 < y2, lower, upper)
-            for b0 in (0, 1):
-                u = spread(v, 1, b0)
-                for b1 in (0, 1):
-                    f = spread(u, 2, b1)
-                    F2[4 * s + 2 * b1 + b0, 8 * m : 8 * m + 8, :] = f
-                    P2A[4 * s + 2 * b1 + b0, 8 * m : 8 * m + 8, :] = -WEIGHT * f
-    rows2 = 4 * (2 * REACH + 1)
-    sweep(P2A, P2B, F2, 1, rows2 - 1, 1, 4)
-
-    def coarse_source(i):
-        v = residual(P2B, F2, 2 * i, 1, 4) + residual(P2B, F2, 2 * i + 1, 1, 4)
-        f = 0.5 * pair(pair(v, 4, 1), 1, 0)
-        return [(F3, i, f), (P3A, i, -WEIGHT * f)]
-
-    loop(1, rows2 // 2 - 1, coarse_source, rows2 // 2 - 2)
-    sweep(P3A, P3B, F3, 2, 16, 2, 8)
-    sweep(P3B, P3A, F3, 3, 15, 2, 8)
-    sweep(P3A, P3B, F3, 4, 14, 2, 8)
-
-    def line_row(r):
-        mean = jnp.mean(residual(P3B, F3, r, 2, 8), axis=0, keepdims=True)
-        v = P3B[r] - WEIGHT * mean
-        return [(P2B, x, P2B[x] + v) for x in (2 * r, 2 * r + 1)]
-
-    loop(6, 12, line_row, 6)
+    known = set()
+    done.update({"first": set(), "second": set(), "base": set()})
+
+    def refine(copies, low, high):
+        finish(copies)
+        known.update(range(low, high))
+        run("first", range(1, wide - 1), lambda r: around_of(r) <= known,
+            lambda r: [(X1, r, smooth(R0, r, 1, 1))], G_FINE)
+        run("second", range(2, wide - 2), lambda r: around_of(r) <= done["first"],
+            lambda r: [(X2, r, smooth(X1, r, 1, 1))], G_FINE)
+        run("base", range(3, wide - 3), lambda r: around_of(r) <= done["second"], base_row, G_FINE)
+
+    refine(face_copies, RIM, RIM + own_x)
+    refine(left_copies, 0, RIM)
+    refine(right_copies, RIM + own_x, wide)
     finish(g_copies)
     full1 = ny * y1
     count1 = packs + 2 * kept
@@ -533,6 +497,82 @@
                 F1[r, k * y1 : (k + 1) * y1, :] = f
                 P1A[r, k * y1 : (k + 1) * y1, :] = -WEIGHT * f
     sweep(P1A, P1B, F1, 1, 2 * count1 - 1, 1, 2)
+    finish(h_copies)
+    full2 = ny * y2
+    blank8 = jnp.zeros((y1, nz), F32)
+    ends = (0, 2 * REACH)
+
+    def spill(k, s):
+        return G2[k, s, 0 if s in ends else 1]
+
+    def joined2(k, s):
+        before = spill(k, s - 1) if s > 0 else blank8
+        after = spill(k, s + 1) if s < 2 * REACH else blank8
+        return G2[k, s, 0] + jnp.where(low2, before, after)
+
+    for s in range(2 * REACH + 1):
+        frames = [joined2(k, s) for k in range(ny)]
+        turned = [roll(v, y2, 0) for v in frames]
+        for m in range(ny // 2):
+            k = 2 * m
+            if ny == 2:
+                v = frames[0] + turned[1]
+            else:
+                lower = frames[k] + jnp.where(sub8 < 2, turned[(k - 1) % ny], turned[(k + 1) % ny])
+                upper = turned[k + 1] + jnp.where(sub8 < 6, frames[k], frames[(k + 2) % ny])
+                v = jnp.where(sub8 < y2, lower, upper)
+            moved = {by: roll(v, by, 1) if by else v for by in range(-3, 4)}
+            for row in range(4):
+                f = moved[-row]
+                for at in range(1, 4):
+                    f = jnp.where(lane8 % 4 == at, moved[at - row], f)
+                F2[4 * s + row, 8 * m : 8 * m + 8, :] = f
+    rows2 = 4 * (2 * REACH + 1)
+    middle2 = range(12, rows2 - 12)
+
+    def level2_row(r):
+        v = smooth(F2, r, 1, 4)
+        stores = [(P2A, r, v)]
+        if r in middle2:
+            stores.append((P2B, r, -WEIGHT * (F2[r] + v)))
+        return stores
+
+    loop(3, rows2 - 3, level2_row, rows2 - 6)
+    rows3 = rows2 // 2
+
+    def coarse_source(i):
+        p = P2A[2 * i] + P2A[2 * i + 1]
+        line = row_of(p.shape[0], nz) % 2 == 0
+        up, down = roll(p, -1, 0), roll(p, 1, 0)
+        pairs = p + jnp.where(line, up, down)
+        beside = P2A[2 * i - 1] + P2A[2 * i + 2]
+        sides = pairs + jnp.where(line, down + roll(p, -2, 0), up + roll(p, 2, 0))
+        beside = beside + jnp.where(line, roll(beside, -1, 0), roll(beside, 1, 0))
+        lanes = lane_of(p.shape[0], nz)
+        inner = KEEP * pairs + WEIGHT * (pairs + beside + sides)
+        low = (lanes // 4) % 2 == 0
+        inner = inner + jnp.where(low, roll(inner, -4, 1), roll(inner, 4, 1))
+        above = jnp.where(lanes >= nz - 4, pairs, roll(pairs, -4, 1))
+        below = jnp.where(lanes < 4, pairs, roll(pairs, 4, 1))
+        above2 = jnp.where(lanes >= nz - 8, above, roll(pairs, -8, 1))
+        below2 = jnp.where(lanes < 8, below, roll(pairs, 8, 1))
+        outer = pairs + above + below + jnp.where(low, above2, below2)
+        return [(F3, i, 0.5 * (inner + 4.0 * WEIGHT * outer))]
+
+    loop(2, rows3 - 2, coarse_source, rows3 - 4)
+    smooth_all(F3, P3A, 3, rows3 - 3, 2, 8)
+    smooth_all(P3A, P3B, 4, rows3 - 4, 2, 8)
+    smooth_all(P3B, P3C, 5, rows3 - 5, 2, 8)
+
+    def line_row(r):
+        left = smooth(P3C, r, 2, 8)
+        eight = sum(left[8 * m : 8 * m + 8] for m in range(full2 // 8))
+        four = eight + roll(eight, 2, 0) + roll(eight, 4, 0) + roll(eight, 6, 0)
+        mean = jnp.concatenate([(2.0 / full2) * four] * (full2 // 8), axis=0)
+        v = -WEIGHT * (F3[r] + P3A[r] + P3B[r] + P3C[r] + mean)
+        return [(P2B, x, P2B[x] + v) for x in (2 * r, 2 * r + 1)]
+
+    loop(6, rows3 - 6, line_row, rows3 - 12)
     sweep(P2B, P2A, F2, 13, 23, 1, 4)
 
     def second_row(m):
@@ -565,8 +605,8 @@
             (Y1, 2 * e - 1, base + WEIGHT * E0[e + 1]),
         ]
 
-    loop(1, 11, first_pair, 5)
-    loop(1, own_x + 3, lambda r: [(PN, r - 1, A[r - 1] + smooth(Y1, r, 1, 1))], 6)
+    loop(1, 11, first_pair, 10)
+    loop(1, own_x + 3, lambda r: [(PN, r - 1, A[r - 1] + smooth(Y1, r, 1, 1))], own_x + 2)
     await_lines(send_sem.at[0], sum(sent))
 
 
@@ -624,12 +664,12 @@
         frame1, window(half + 10, 2 * y1), window(ny, packs + 10, y1 + 2),
         level1, level1, level1,
         window(ny, 2 * REACH + 1, 2, y1), window(2, y1),
-        level2, level2, level2, level3, level3, level3,
+        level2, level2, level2, level3, level3, level3, level3,
         window(8, full1), window(12, side),
         window(total),
         pltpu.SemaphoreType.DMA((5,)),
         pltpu.SemaphoreType.DMA((1,)),
-        pltpu.SemaphoreType.DMA((11,)),
+        pltpu.SemaphoreType.DMA((13,)),
         pltpu.SemaphoreType.REGULAR((6,)),
     ]
     inside = pl.BlockSpec(memory_space=pltpu.VMEM)

time: 21.5 us -> 20.9 us (0.972)
  Pallas kernels: 20.8 us -> 20.1 us
    pallas_call x1, Pallas kernels: 19.9 us -> 19.3 us  [per_device(): pl.pallas_call(functools.partial(kernel, nx, ny), out_shape=(jax.ShapeDty...]
where the time goes in v5:
time: 20.9 us; the launch traced here: 20.8 us
  Pallas kernels  20.1 us (96%)
  between operations  0.64 us (3%)
    pallas_call x1, Pallas kernels, per_device(): pl.pallas_call(functools.partial(kernel, nx, ny), out_shape=(jax.ShapeDty...  19.3 us
    pallas_call x1, Pallas kernels, per_device(): pl.pallas_call(closing, out_shape=(jax.ShapeDtypeStruct(velocity.shape, F...  0.88 us

profile of v5, /device:TPU:0, one launch (start us, length us, event | category | flops | bytes accessed | tf_op | source)
XLA Modules:
  0.0 20.8 jit_solution(8691784314278952034)
XLA Ops:
  0.6 19.3 %shard_map.68 = (f32[3,22,24,128]{3,2,1,0:T(8,128)S(1)}, f32[18,24,128]{2,1,0:T(8,128)S(1)}) custom-call(f32[3,16,16,128]{3,2,1,0:T(8,128)} %vel_in.1, f32[16,16,128]{2,1,0:T(8,128)} %pre_in.1, s32[16,16,128]{2,1,0:T(8,128)} %turb_in.1, s32[16,16]{1,0:T(8,128)} %land_in.1, f32[16]{0:T(128)} %coeff_in.1), custom_call_target="tpu_custom_call" | custom-call | tf_op jit(solution)/shard_map/pallas_call | solution.py:681
  19.9 0.9 %shard_map.69 = (f32[3,16,16,128]{3,2,1,0:T(8,128)}, f32[16,16,128]{2,1,0:T(8,128)}) custom-call(f32[3,22,24,128]{3,2,1,0:T(8,128)S(1)} %get-tuple-element.4.S, f32[18,24,128]{2,1,0:T(8,128)S(1)} %get-tuple-element.5.PN), custom_call_target="tpu_custom_call" | custom-call | tf_op jit(solution)/shard_map/pallas_call | solution.py:694

commit v6 on v5

--- a/solution.py
+++ b/solution.py
@@ -78,7 +78,7 @@
         return (lax.rem(me_x + dx + nx, nx), lax.rem(me_y + dy + ny, ny))
 
     far = [(dx, dy) for dx in range(-REACH, REACH + 1) for dy in range(ny) if dx or dy]
-    close = [(dx, dy) for dx, dy in far if abs(dx) < 2]
+    close = [(dx, dy) for dx, dy in far if dx == 0 or (dy == 0 and abs(dx) < 2)]
     barrier = pltpu.get_barrier_semaphore()
     for dx, dy in close:
         pl.semaphore_signal(barrier, inc=1, device_id=device(dx, dy), device_id_type=MESH)
@@ -145,16 +145,13 @@
         at = turn + (3 if dx < 0 else 0)
         pl.semaphore_signal(token.at[at], inc=1, device_id=device(dx, 0), device_id_type=MESH)
 
-    def hear_right(turn, crosses):
-        end = me_x >= nx - 1 - turn
-
-        @pl.when(end if crosses else jnp.logical_not(end))
-        def _():
-            hear(turn, 1)
+    def listen(turn, crosses):
+        for dx, end in ((1, me_x >= nx - 1 - turn), (-1, me_x <= turn + 1)):
+            pl.when(end if crosses else jnp.logical_not(end))(functools.partial(hear, turn, dx))
 
     pl.semaphore_wait(barrier, len(close))
-    tell(0, 1)
-    tell(0, -1)
+    for dy in range(1, ny):
+        pl.semaphore_signal(token.at[6], inc=1, device_id=device(0, dy), device_id_type=MESH)
     piece = own_x // 4
     low_end, high_end = 2 * piece, own_x - own_x // 8
     middle = (low_end + high_end) // 2
@@ -170,8 +167,6 @@
 
     low_copies, high_copies = group(), group()
     for dx, at in ((-1, high_copies), (1, low_copies)):
-        for dy in (1, -1):
-            send(at, vel_in, W, 0, OFF, 2, dx, dy, True)
         send(at, vel_in, W, 0, OFF, 3, dx, 0, True)
     slabs = [slab(cut) for cut in cuts[:2]]
     shape = (own_y, own_y)
@@ -193,7 +188,14 @@
         at = high_copies if dx == -1 else d_copies
         send(at, D, D, OFF, OFF, 1, dx, dy)
         send(at, pre_in, PA, 0, OFF, 1, dx, dy)
-    slabs += [slab(cut) for cut in cuts[2:]]
+    slabs += [slab(cut) for cut in cuts[2:3]]
+    pl.semaphore_wait(token.at[6], ny - 1)
+    tell(0, 1)
+    tell(0, -1)
+    for dx, at in ((-1, high_copies), (1, low_copies)):
+        for dy in (1, -1):
+            send(at, vel_in, W, 0, OFF, 2, dx, dy, True)
+    slabs += [slab(cut) for cut in cuts[3:]]
     blank = jnp.zeros((side, nz), F32)
     for r in (1, 2, rows - 3, rows - 2):
         Z[r] = blank
@@ -362,24 +364,23 @@
         advance(full)
 
     for turn in range(3):
-        hear_right(turn, False)
-        hear(turn, -1)
+        listen(turn, False)
     arrive(slabs[0], *cuts[0], False)
-    arrive(low_copies, -OFF, 0, False)
     arrive(slabs[1], *cuts[1], False)
     finish(d_copies)
     high_rows = set(range(OFF + own_x, rows))
     behind.update(range(OFF + own_x))
     advance(True)
-    hear_right(0, True)
+    listen(0, True)
     arrive(slabs[2], *cuts[2], True)
-    hear_right(1, True)
+    arrive(low_copies, -OFF, 0, False)
+    listen(1, True)
     arrive(slabs[3], *cuts[3], True)
     while split in done["source"]:
         split += 1
     r0_faces(OFF, split)
     r0_side(-1)
-    hear_right(2, True)
+    listen(2, True)
     finish(high_copies)
     here.update(high_rows)
     behind.update(high_rows)
@@ -429,7 +430,7 @@
     GX[0] = jnp.where(low2, beyond, near)
     GX[1] = jnp.where(low2, near, beyond)
     h_copies = group()
-    order = sorted(far, key=lambda to: (to[0] == 0, abs(to[0]) == 1, -to[0], -to[1]))
+    order = sorted(far, key=lambda to: (to[0] <= 0, to[0] if to[0]>0 else -to[0], -to[1]))
 
     def spread_out(sign):
         for dx, dy in order:
@@ -670,7 +671,7 @@
         pltpu.SemaphoreType.DMA((5,)),
         pltpu.SemaphoreType.DMA((1,)),
         pltpu.SemaphoreType.DMA((13,)),
-        pltpu.SemaphoreType.REGULAR((6,)),
+        pltpu.SemaphoreType.REGULAR((7,)),
     ]
     inside = pl.BlockSpec(memory_space=pltpu.VMEM)
     outside = pl.BlockSpec(memory_space=pltpu.HBM)

time: 20.9 us -> 20.5 us (0.981)
  Pallas kernels: 20.1 us -> 19.7 us
    pallas_call x1, Pallas kernels: 19.3 us -> 18.8 us  [per_device(): pl.pallas_call(functools.partial(kernel, nx, ny), out_shape=(jax.ShapeDty...]
where the time goes in v6:
time: 20.5 us; the launch traced here: 20.3 us
  Pallas kernels  19.7 us (96%)
  between operations  0.64 us (3%)
    pallas_call x1, Pallas kernels, per_device(): pl.pallas_call(functools.partial(kernel, nx, ny), out_shape=(jax.ShapeDty...  18.8 us
    pallas_call x1, Pallas kernels, per_device(): pl.pallas_call(closing, out_shape=(jax.ShapeDtypeStruct(velocity.shape, F...  0.88 us

profile of v6, /device:TPU:0, one launch (start us, length us, event | category | flops | bytes accessed | tf_op | source)
XLA Modules:
  0.0 20.3 jit_solution(1219360051719875547)
XLA Ops:
  0.6 18.8 %shard_map.68 = (f32[3,22,24,128]{3,2,1,0:T(8,128)S(1)}, f32[18,24,128]{2,1,0:T(8,128)S(1)}) custom-call(f32[3,16,16,128]{3,2,1,0:T(8,128)} %vel_in.1, f32[16,16,128]{2,1,0:T(8,128)} %pre_in.1, s32[16,16,128]{2,1,0:T(8,128)} %turb_in.1, s32[16,16]{1,0:T(8,128)} %land_in.1, f32[16]{0:T(128)} %coeff_in.1), custom_call_target="tpu_custom_call" | custom-call | tf_op jit(solution)/shard_map/pallas_call | solution.py:682
  19.4 0.9 %shard_map.69 = (f32[3,16,16,128]{3,2,1,0:T(8,128)}, f32[16,16,128]{2,1,0:T(8,128)}) custom-call(f32[3,22,24,128]{3,2,1,0:T(8,128)S(1)} %get-tuple-element.4.S, f32[18,24,128]{2,1,0:T(8,128)S(1)} %get-tuple-element.5.PN), custom_call_target="tpu_custom_call" | custom-call | tf_op jit(solution)/shard_map/pallas_call | solution.py:695

commit v7 on v6

--- a/solution.py
+++ b/solution.py
@@ -71,7 +71,7 @@
         pltpu.make_async_copy(land_in, land, load_sem.at[1]),
         pltpu.make_async_copy(coeff_in, coeff, load_sem.at[2]),
         pltpu.make_async_copy(vel_in, W.at[:, OFF : OFF + own_x, 0:own_y], load_sem.at[3]),
-        pltpu.make_async_copy(pre_in, PA.at[OFF : OFF + own_x, 0:own_y], load_sem.at[4]),
+        pltpu.make_async_copy(pre_in, PA.at[OFF : OFF + own_x, 0:own_y], load_sem.at[3]),
     ]
 
     def device(dx, dy):
@@ -155,6 +155,7 @@
     piece = own_x // 4
     low_end, high_end = 2 * piece, own_x - own_x // 8
     middle = (low_end + high_end) // 2
+    middle -= 1
     cuts = [(0, piece), (piece, low_end), (low_end, middle), (middle, high_end), (high_end, own_x)]
 
     def slab(cut):
@@ -206,8 +207,7 @@
         H1[r] = blank1
     for r in (0, 1, 2, half + 7, half + 8, half + 9):
         H1A[r] = blank1
-    loads[3].wait()
-    loads[4].wait()
+    await_lines(load_sem.at[3], lines_of(vel_in) + lines_of(pre_in))
     lane = lane_of(side, nz)
     first, last = lane == 0, lane == nz - 1
 
@@ -466,8 +466,8 @@
         run("base", range(3, wide - 3), lambda r: around_of(r) <= done["second"], base_row, G_FINE)
 
     refine(face_copies, RIM, RIM + own_x)
+    refine(right_copies, RIM + own_x, wide)
     refine(left_copies, 0, RIM)
-    refine(right_copies, RIM + own_x, wide)
     finish(g_copies)
     full1 = ny * y1
     count1 = packs + 2 * kept
@@ -668,7 +668,7 @@
         level2, level2, level2, level3, level3, level3, level3,
         window(8, full1), window(12, side),
         window(total),
-        pltpu.SemaphoreType.DMA((5,)),
+        pltpu.SemaphoreType.DMA((4,)),
         pltpu.SemaphoreType.DMA((1,)),
         pltpu.SemaphoreType.DMA((13,)),
         pltpu.SemaphoreType.REGULAR((7,)),

time: 20.5 us -> 20.5 us (level)
  no operation moved by 1% of the time
where the time goes in v7:
time: 20.5 us; the launch traced here: 20.4 us
  Pallas kernels  19.7 us (96%)
  between operations  0.64 us (3%)
    pallas_call x1, Pallas kernels, per_device(): pl.pallas_call(functools.partial(kernel, nx, ny), out_shape=(jax.ShapeDty...  18.8 us
    pallas_call x1, Pallas kernels, per_device(): pl.pallas_call(closing, out_shape=(jax.ShapeDtypeStruct(velocity.shape, F...  0.88 us

profile of v7, /device:TPU:0, one launch (start us, length us, event | category | flops | bytes accessed | tf_op | source)
XLA Modules:
  0.0 20.4 jit_solution(15533717731218873906)
XLA Ops:
  0.6 18.8 %shard_map.68 = (f32[3,22,24,128]{3,2,1,0:T(8,128)S(1)}, f32[18,24,128]{2,1,0:T(8,128)S(1)}) custom-call(f32[3,16,16,128]{3,2,1,0:T(8,128)} %vel_in.1, f32[16,16,128]{2,1,0:T(8,128)} %pre_in.1, s32[16,16,128]{2,1,0:T(8,128)} %turb_in.1, s32[16,16]{1,0:T(8,128)} %land_in.1, f32[16]{0:T(128)} %coeff_in.1), custom_call_target="tpu_custom_call" | custom-call | tf_op jit(solution)/shard_map/pallas_call | solution.py:682
  19.5 0.9 %shard_map.69 = (f32[3,16,16,128]{3,2,1,0:T(8,128)}, f32[16,16,128]{2,1,0:T(8,128)}) custom-call(f32[3,22,24,128]{3,2,1,0:T(8,128)S(1)} %get-tuple-element.4.S, f32[18,24,128]{2,1,0:T(8,128)S(1)} %get-tuple-element.5.PN), custom_call_target="tpu_custom_call" | custom-call | tf_op jit(solution)/shard_map/pallas_call | solution.py:695
